TPU v7x, 512 devices: a whole 4x8x8 slice. The times are simulated.
512 devices in a mesh: lon: 64 (over z, y_lo, core), lat: 8 (over x, y_hi).
Axes of the slice: x: 4, y: 8 (y_hi: 2, y_lo: 4; y = y_hi * 4 + y_lo), z: 8, core: 2. Of those that a mesh axis runs over, the one named last changes fastest.
Arguments:
- pressure: float32 [128, 1024, 1024], P(None, 'lon', 'lat'), may hold values from -10 to 10
- ocean_mask: int32 [1024, 1024], P('lon', 'lat'), may hold values 0 or 1
Outputs:
- modes: float32 [128, 3, 1024, 1024], P(None, None, 'lon', 'lat')
- factor_r: float32 [128, 128], replicated
All inputs are finite; a program needn't handle non-finite values. No bound on the sum of `ocean_mask` on one device may be relied on, other than what follows from the above.
Results may differ from a plain program's by a relative error of at most 0.0003.
Values sent between devices are 32-bit elements; how exact they have to be, the bound alone decides.
A program may use at most 64 MiB of HBM per device.

v0:
```python
import jax
import jax.numpy as jnp
from jax import lax
from jax.sharding import PartitionSpec as P

PASSES = 4


def extended(block, sides, width, periodic):
    for axis, dim in sides:
        count = lax.axis_size(axis)
        forward = [(i, i + 1) for i in range(count - 1)]
        if periodic:
            forward.append((count - 1, 0))
        backward = [(target, source) for source, target in forward]
        low = lax.ppermute(
            lax.slice_in_dim(block, block.shape[dim] - width, None, axis=dim), axis, forward
        )
        high = lax.ppermute(lax.slice_in_dim(block, 0, width, axis=dim), axis, backward)
        block = jnp.concatenate([low, block, high], axis=dim)
    return block


def sweep_lon(ext, mask_ext):
    center = ext[:, 1:-1, :]
    mask_mid = mask_ext[1:-1, :]
    return mask_mid * (
        center
        + 0.25
        * (
            mask_ext[:-2, :] * (ext[:, :-2, :] - center)
            + mask_ext[2:, :] * (ext[:, 2:, :] - center)
        )
    )


def sweep_lat(ext, mask_ext):
    center = ext[:, :, 1:-1]
    mask_mid = mask_ext[:, 1:-1]
    return mask_mid * (
        center
        + 0.25
        * (
            mask_ext[:, :-2] * (ext[:, :, :-2] - center)
            + mask_ext[:, 2:] * (ext[:, :, 2:] - center)
        )
    )


def rim_lon(field):
    return extended(field, (("lon", 1),), 1, True)


def rim_lat(field):
    return extended(field, (("lat", 2),), 1, False)


def orthonormalize(flat):
    local_gram = lax.dot_general(
        flat,
        flat,
        (((1,), (1,)), ((), ())),
        precision=lax.Precision.HIGHEST,
        preferred_element_type=jnp.float32,
    )
    gram = lax.psum(local_gram, ("lon", "lat"))
    lower = jnp.linalg.cholesky(gram)
    eye = jnp.eye(gram.shape[0], dtype=jnp.float32)
    inverse = jax.scipy.linalg.solve_triangular(lower, eye, lower=True)
    return (
        jnp.dot(inverse, flat, precision=lax.Precision.HIGHEST, preferred_element_type=jnp.float32),
        lower,
    )


def on_device(pressure, ocean_mask):
    margin = PASSES + 1
    clon, clat = ocean_mask.shape
    mask_wide = extended(ocean_mask, (("lon", 0),), margin, True)
    mask_wide = extended(mask_wide, (("lat", 1),), margin, False).astype(jnp.float32)
    inner = mask_wide[margin : margin + clon, margin : margin + clat]
    field = inner * pressure
    mask_one = mask_wide[margin - 1 : margin + clon + 1, margin - 1 : margin + clat + 1]
    for step in range(PASSES):
        field = sweep_lon(rim_lon(field), mask_one[:, 1:-1])
        field = sweep_lat(rim_lat(field), mask_one[1:-1, :])
    lon_ext = rim_lon(field)
    lat_ext = rim_lat(field)
    grad_lon = 0.5 * inner * (lon_ext[:, 2:, :] - lon_ext[:, :-2, :])
    grad_lat = 0.5 * inner * (lat_ext[:, :, 2:] - lat_ext[:, :, :-2])
    stacked = jnp.stack([field, grad_lon, grad_lat], axis=1)
    snaps = stacked.shape[0]
    flat = stacked.reshape(snaps, -1)
    first, lower_one = orthonormalize(flat)
    second, lower_two = orthonormalize(first)
    total_rows = 3 * clon * clat * lax.axis_size("lon") * lax.axis_size("lat")
    scale = jnp.sqrt(jnp.float32(total_rows))
    modes = (second * scale).reshape(snaps, 3, clon, clat)
    factor_r = (
        jnp.dot(
            lower_two.T,
            lower_one.T,
            precision=lax.Precision.HIGHEST,
            preferred_element_type=jnp.float32,
        )
        / scale
    )
    return (modes, factor_r)


def solution(mesh):
    return jax.shard_map(
        on_device,
        mesh=mesh,
        in_specs=(P(None, "lon", "lat"), P("lon", "lat")),
        out_specs=(P(None, None, "lon", "lat"), P()),
        check_vma=False,
    )
```

profile of v0, /device:TPU:1, one launch (start us, length us, event | category | flops | bytes accessed | tf_op | source)
XLA Modules:
  0.0 785.4 jit_solution(9866889213399363693)
XLA Ops:
  7.9 4.6 collective-permute-start
  12.5 6.1 collective-permute-start.1
  20.2 4.6 collective-permute-start.2
  26.1 7.1 collective-permute-done.3
  34.0 1.6 copy_multiply_fusion
  35.6 3.5 collective-permute-start.4
  39.1 8.6 %collective-permute-start.5 = (f32[128,1,128]{2,0,1:T(8,128)S(1)}, f32[128,1,128]{2,0,1:T(8,128)S(1)}, u32[]{:S(2)}, u32[]{:S(2)}) collective-permute-start(f32[128,1,128]{2,0,1:T(8,128)S(1)} %get-tuple-element.25), channel_id=1, source_target_pairs={{8,0},{16,8},{24,16},{32,24},{40,32},{48,40},{56,48},{64,56},{72,6... | collective-permute-start | bytes 196616 | tf_op jit(solution)/shard_map/ppermute | solution.py:19
  49.6 6.3 collective-permute-start.6
  56.2 1.3 collective-permute-start.7
  57.9 6.6 collective-permute-done.7
  65.8 1.9 collective-permute-start.8
  67.7 10.1 %collective-permute-start.9 = (f32[128,1,128]{2,0,1:T(8,128)S(1)}, f32[128,1,128]{2,0,1:T(8,128)S(1)}, u32[]{:S(2)}, u32[]{:S(2)}) collective-permute-start(f32[128,1,128]{2,0,1:T(8,128)S(1)} %get-tuple-element.21), channel_id=1, source_target_pairs={{8,0},{16,8},{24,16},{32,24},{40,32},{48,40},{56,48},{64,56},{72,6... | collective-permute-start | bytes 196616 | tf_op jit(solution)/shard_map/ppermute | solution.py:19
  79.6 4.7 collective-permute-start.10
  84.7 1.3 collective-permute-start.11
  86.3 6.6 collective-permute-done.11
  94.2 1.9 collective-permute-start.12
  96.2 10.0 %collective-permute-start.13 = (f32[128,1,128]{2,0,1:T(8,128)S(1)}, f32[128,1,128]{2,0,1:T(8,128)S(1)}, u32[]{:S(2)}, u32[]{:S(2)}) collective-permute-start(f32[128,1,128]{2,0,1:T(8,128)S(1)} %get-tuple-element.17), channel_id=1, source_target_pairs={{8,0},{16,8},{24,16},{32,24},{40,32},{48,40},{56,48},{64,56},{72,6... | collective-permute-start | bytes 196616 | tf_op jit(solution)/shard_map/ppermute | solution.py:19
  108.0 6.3 collective-permute-start.14
  116.4 6.6 collective-permute-done.15
  124.3 1.9 collective-permute-start.16
  126.2 10.1 %collective-permute-start.17 = (f32[128,1,128]{2,0,1:T(8,128)S(1)}, f32[128,1,128]{2,0,1:T(8,128)S(1)}, u32[]{:S(2)}, u32[]{:S(2)}) collective-permute-start(f32[128,1,128]{2,0,1:T(8,128)S(1)} %get-tuple-element.13), channel_id=1, source_target_pairs={{8,0},{16,8},{24,16},{32,24},{40,32},{48,40},{56,48},{64,56},{72,6... | collective-permute-start | bytes 196616 | tf_op jit(solution)/shard_map/ppermute | solution.py:19
  138.2 4.8 collective-permute-start.18
  145.0 6.6 collective-permute-done.19
  151.6 1.3 copy.31
  152.9 2.1 fusion.12
  155.1 1.7 fusion.94
  156.8 10.0 %collective-permute-start.20 = (f32[128,1,128]{2,0,1:T(8,128)S(1)}, f32[128,1,128]{2,0,1:T(8,128)S(1)}, u32[]{:S(2)}, u32[]{:S(2)}) collective-permute-start(f32[128,1,128]{2,0,1:T(8,128)S(1)} %get-tuple-element.6), channel_id=1, source_target_pairs={{8,0},{16,8},{24,16},{32,24},{40,32},{48,40},{56,48},{64,56},{72,6... | collective-permute-start | bytes 196616 | tf_op jit(solution)/shard_map/ppermute | solution.py:19
  166.7 1.9 collective-permute-start.21
  168.7 1.6 copy.32
  170.2 1.6 copy.34
  171.8 6.1 collective-permute-start.23
  177.9 1.6 collective-permute-start.22
  179.5 3.1 fusion.113
  182.6 3.5 collective-permute-done.22
  189.2 3.2 convolution_bitcast_fusion
  192.5 2.1 pad_maximum_fusion
  194.6 2.4 copy.38
  196.9 260.4 %all-reduce.3.cloned.1.call-done = f32[128,128]{0,1:T(8,128)} async-done(((f32[128,128]{0,1:T(8,128)}), f32[128,128]{0,1:T(8,128)}) %all-reduce.3.cloned.1.call-update) | async-done | bytes 65552 | tf_op jit(solution)/shard_map/psum | solution.py:66
  459.2 11.7 %cholesky.44 = f32[128,128]{1,0:T(8,128)S(1)} custom-call(f32[128,128]{1,0:T(8,128)S(1)} %fusion.78), custom_call_target="Cholesky" | custom-call | tf_op jit(solution)/shard_map/jit(cholesky)/cholesky | solution.py:67
  472.3 9.8 %custom-call.6 = f32[1,128,128]{1,2,0:T(8,128)S(1)} custom-call(f32[1,128,128]{2,1,0:T(8,128)S(1)} %fusion.82), custom_call_target="InvertDiagBlocksLowerTriangular" | custom-call | tf_op jit(solution)/shard_map/jit(_solve_triangular)/triangular_solve | solution.py:69
  482.4 4.7 fusion.105
  487.0 3.2 fusion.106
  490.3 255.5 %all-reduce.5.cloned.1.call-done = f32[128,128]{0,1:T(8,128)} async-done(((f32[128,128]{0,1:T(8,128)}), f32[128,128]{0,1:T(8,128)}) %all-reduce.5.cloned.1.call-update) | async-done | bytes 65552 | tf_op jit(solution)/shard_map/psum | solution.py:66
  747.6 11.9 %cholesky.55 = f32[128,128]{1,0:T(8,128)S(1)} custom-call(f32[128,128]{1,0:T(8,128)S(1)} %fusion.76), custom_call_target="Cholesky" | custom-call | tf_op jit(solution)/shard_map/jit(cholesky)/cholesky | solution.py:67
  760.2 2.2 convolution_multiply_fusion.1
  763.0 9.8 %custom-call.7 = f32[1,128,128]{1,2,0:T(8,128)S(1)} custom-call(f32[1,128,128]{2,1,0:T(8,128)S(1)} %select_bitcast_fusion), custom_call_target="InvertDiagBlocksLowerTriangular" | custom-call | tf_op jit(solution)/shard_map/jit(_solve_triangular)/triangular_solve | solution.py:69
  773.1 3.0 fusion
  776.1 2.2 copy.44
  (82 shorter events, 31.0 us)
Async XLA Ops:
  7.2 450.2 %all-reduce.3.cloned.1.call-start = ((), (), s32[]{:S(2)}) async-start(), calls=%async_computation | async-start | bytes 131072 | tf_op jit(solution)/shard_map/psum | solution.py:66
  7.9 10.7 %collective-permute-start = (s32[5,128]{1,0:T(8,128)S(1)}, s32[5,128]{1,0:T(8,128)S(1)}, u32[]{:S(2)}, u32[]{:S(2)}) collective-permute-start(s32[5,128]{1,0:T(8,128)S(1)} %get-tuple-element.34), channel_id=1, source_target_pairs={{0,8},{8,16},{16,24},{24,32},{32,40},{40,48},{48,56},{56,64},{64,7... | collective-permute-start | bytes 7688 | tf_op jit(solution)/shard_map/ppermute | solution.py:16
  12.5 6.9 collective-permute-start.1
  20.2 5.9 collective-permute-start.2
  24.8 8.4 %collective-permute-start.3 = (s32[26,5]{1,0:T(8,128)S(1)}, s32[26,5]{1,0:T(8,128)S(1)}, u32[]{:S(2)}, u32[]{:S(2)}) collective-permute-start(s32[26,5]{1,0:T(8,128)S(1)} %get-tuple-element.33), channel_id=1, source_target_pairs={{1,0},{2,1},{3,2},{4,3},{5,4},{6,5},{7,6},{9,8},{10,9},{11,10},{12... | collective-permute-start | bytes 1568 | tf_op jit(solution)/shard_map/ppermute | solution.py:19
  35.6 12.1 %collective-permute-start.4 = (f32[128,1,128]{2,0,1:T(8,128)S(1)}, f32[128,1,128]{2,0,1:T(8,128)S(1)}, u32[]{:S(2)}, u32[]{:S(2)}) collective-permute-start(f32[128,1,128]{2,0,1:T(8,128)S(1)} %get-tuple-element.24), channel_id=1, source_target_pairs={{0,8},{8,16},{16,24},{24,32},{32,40},{40,48},{48,56},{56,64},{64,7... | collective-permute-start | bytes 196616 | tf_op jit(solution)/shard_map/ppermute | solution.py:16
  39.1 9.5 %collective-permute-start.5 = (f32[128,1,128]{2,0,1:T(8,128)S(1)}, f32[128,1,128]{2,0,1:T(8,128)S(1)}, u32[]{:S(2)}, u32[]{:S(2)}) collective-permute-start(f32[128,1,128]{2,0,1:T(8,128)S(1)} %get-tuple-element.25), channel_id=1, source_target_pairs={{8,0},{16,8},{24,16},{32,24},{40,32},{48,40},{56,48},{64,56},{72,6... | collective-permute-start | bytes 196616 | tf_op jit(solution)/shard_map/ppermute | solution.py:19
  49.6 7.9 %collective-permute-start.6 = (f32[128,16,1]{0,1,2:T(8,128)S(1)}, f32[128,16,1]{0,1,2:T(8,128)S(1)}, u32[]{:S(2)}, u32[]{:S(2)}) collective-permute-start(f32[128,16,1]{0,1,2:T(8,128)S(1)} %copy.16), channel_id=1, source_target_pairs={{0,1},{1,2},{2,3},{3,4},{4,5},{5,6},{6,7},{8,9},{9,10},{10,11},{11... | collective-permute-start | bytes 24584 | tf_op jit(solution)/shard_map/ppermute | solution.py:16
  56.2 8.3 %collective-permute-start.7 = (f32[128,16,1]{0,1,2:T(8,128)S(1)}, f32[128,16,1]{0,1,2:T(8,128)S(1)}, u32[]{:S(2)}, u32[]{:S(2)}) collective-permute-start(f32[128,16,1]{0,1,2:T(8,128)S(1)} %copy.18), channel_id=1, source_target_pairs={{1,0},{2,1},{3,2},{4,3},{5,4},{6,5},{7,6},{9,8},{10,9},{11,10},{12... | collective-permute-start | bytes 24584 | tf_op jit(solution)/shard_map/ppermute | solution.py:19
  65.8 12.0 %collective-permute-start.8 = (f32[128,1,128]{2,0,1:T(8,128)S(1)}, f32[128,1,128]{2,0,1:T(8,128)S(1)}, u32[]{:S(2)}, u32[]{:S(2)}) collective-permute-start(f32[128,1,128]{2,0,1:T(8,128)S(1)} %get-tuple-element.20), channel_id=1, source_target_pairs={{0,8},{8,16},{16,24},{24,32},{32,40},{40,48},{48,56},{56,64},{64,7... | collective-permute-start | bytes 196616 | tf_op jit(solution)/shard_map/ppermute | solution.py:16
  67.7 11.0 %collective-permute-start.9 = (f32[128,1,128]{2,0,1:T(8,128)S(1)}, f32[128,1,128]{2,0,1:T(8,128)S(1)}, u32[]{:S(2)}, u32[]{:S(2)}) collective-permute-start(f32[128,1,128]{2,0,1:T(8,128)S(1)} %get-tuple-element.21), channel_id=1, source_target_pairs={{8,0},{16,8},{24,16},{32,24},{40,32},{48,40},{56,48},{64,56},{72,6... | collective-permute-start | bytes 196616 | tf_op jit(solution)/shard_map/ppermute | solution.py:19
  79.6 6.3 collective-permute-start.10
  84.7 8.3 %collective-permute-start.11 = (f32[128,16,1]{0,1,2:T(8,128)S(1)}, f32[128,16,1]{0,1,2:T(8,128)S(1)}, u32[]{:S(2)}, u32[]{:S(2)}) collective-permute-start(f32[128,16,1]{0,1,2:T(8,128)S(1)} %copy.22), channel_id=1, source_target_pairs={{1,0},{2,1},{3,2},{4,3},{5,4},{6,5},{7,6},{9,8},{10,9},{11,10},{12... | collective-permute-start | bytes 24584 | tf_op jit(solution)/shard_map/ppermute | solution.py:19
  94.2 11.9 %collective-permute-start.12 = (f32[128,1,128]{2,0,1:T(8,128)S(1)}, f32[128,1,128]{2,0,1:T(8,128)S(1)}, u32[]{:S(2)}, u32[]{:S(2)}) collective-permute-start(f32[128,1,128]{2,0,1:T(8,128)S(1)} %get-tuple-element.16), channel_id=1, source_target_pairs={{0,8},{8,16},{16,24},{24,32},{32,40},{40,48},{48,56},{56,64},{64,7... | collective-permute-start | bytes 196616 | tf_op jit(solution)/shard_map/ppermute | solution.py:16
  96.2 10.9 %collective-permute-start.13 = (f32[128,1,128]{2,0,1:T(8,128)S(1)}, f32[128,1,128]{2,0,1:T(8,128)S(1)}, u32[]{:S(2)}, u32[]{:S(2)}) collective-permute-start(f32[128,1,128]{2,0,1:T(8,128)S(1)} %get-tuple-element.17), channel_id=1, source_target_pairs={{8,0},{16,8},{24,16},{32,24},{40,32},{48,40},{56,48},{64,56},{72,6... | collective-permute-start | bytes 196616 | tf_op jit(solution)/shard_map/ppermute | solution.py:19
  108.0 8.0 %collective-permute-start.14 = (f32[128,16,1]{0,1,2:T(8,128)S(1)}, f32[128,16,1]{0,1,2:T(8,128)S(1)}, u32[]{:S(2)}, u32[]{:S(2)}) collective-permute-start(f32[128,16,1]{0,1,2:T(8,128)S(1)} %copy.24), channel_id=1, source_target_pairs={{0,1},{1,2},{2,3},{3,4},{4,5},{5,6},{6,7},{8,9},{9,10},{10,11},{11... | collective-permute-start | bytes 24584 | tf_op jit(solution)/shard_map/ppermute | solution.py:16
  114.7 8.3 %collective-permute-start.15 = (f32[128,16,1]{0,1,2:T(8,128)S(1)}, f32[128,16,1]{0,1,2:T(8,128)S(1)}, u32[]{:S(2)}, u32[]{:S(2)}) collective-permute-start(f32[128,16,1]{0,1,2:T(8,128)S(1)} %copy.26), channel_id=1, source_target_pairs={{1,0},{2,1},{3,2},{4,3},{5,4},{6,5},{7,6},{9,8},{10,9},{11,10},{12... | collective-permute-start | bytes 24584 | tf_op jit(solution)/shard_map/ppermute | solution.py:19
  124.3 12.0 %collective-permute-start.16 = (f32[128,1,128]{2,0,1:T(8,128)S(1)}, f32[128,1,128]{2,0,1:T(8,128)S(1)}, u32[]{:S(2)}, u32[]{:S(2)}) collective-permute-start(f32[128,1,128]{2,0,1:T(8,128)S(1)} %get-tuple-element.12), channel_id=1, source_target_pairs={{0,8},{8,16},{16,24},{24,32},{32,40},{40,48},{48,56},{56,64},{64,7... | collective-permute-start | bytes 196616 | tf_op jit(solution)/shard_map/ppermute | solution.py:16
  126.2 11.0 %collective-permute-start.17 = (f32[128,1,128]{2,0,1:T(8,128)S(1)}, f32[128,1,128]{2,0,1:T(8,128)S(1)}, u32[]{:S(2)}, u32[]{:S(2)}) collective-permute-start(f32[128,1,128]{2,0,1:T(8,128)S(1)} %get-tuple-element.13), channel_id=1, source_target_pairs={{8,0},{16,8},{24,16},{32,24},{40,32},{48,40},{56,48},{64,56},{72,6... | collective-permute-start | bytes 196616 | tf_op jit(solution)/shard_map/ppermute | solution.py:19
  138.2 6.4 collective-permute-start.18
  143.3 8.3 %collective-permute-start.19 = (f32[128,16,1]{0,1,2:T(8,128)S(1)}, f32[128,16,1]{0,1,2:T(8,128)S(1)}, u32[]{:S(2)}, u32[]{:S(2)}) collective-permute-start(f32[128,16,1]{0,1,2:T(8,128)S(1)} %copy.30), channel_id=1, source_target_pairs={{1,0},{2,1},{3,2},{4,3},{5,4},{6,5},{7,6},{9,8},{10,9},{11,10},{12... | collective-permute-start | bytes 24584 | tf_op jit(solution)/shard_map/ppermute | solution.py:19
  156.8 30.2 %collective-permute-start.20 = (f32[128,1,128]{2,0,1:T(8,128)S(1)}, f32[128,1,128]{2,0,1:T(8,128)S(1)}, u32[]{:S(2)}, u32[]{:S(2)}) collective-permute-start(f32[128,1,128]{2,0,1:T(8,128)S(1)} %get-tuple-element.6), channel_id=1, source_target_pairs={{8,0},{16,8},{24,16},{32,24},{40,32},{48,40},{56,48},{64,56},{72,6... | collective-permute-start | bytes 196616 | tf_op jit(solution)/shard_map/ppermute | solution.py:19
  166.7 20.2 %collective-permute-start.21 = (f32[128,1,128]{2,0,1:T(8,128)S(1)}, f32[128,1,128]{2,0,1:T(8,128)S(1)}, u32[]{:S(2)}, u32[]{:S(2)}) collective-permute-start(f32[128,1,128]{2,0,1:T(8,128)S(1)} %get-tuple-element.7), channel_id=1, source_target_pairs={{0,8},{8,16},{16,24},{24,32},{32,40},{40,48},{48,56},{56,64},{64,7... | collective-permute-start | bytes 196616 | tf_op jit(solution)/shard_map/ppermute | solution.py:16
  171.8 14.8 %collective-permute-start.23 = (f32[128,16,1]{0,1,2:T(8,128)S(1)}, f32[128,16,1]{0,1,2:T(8,128)S(1)}, u32[]{:S(2)}, u32[]{:S(2)}) collective-permute-start(f32[128,16,1]{0,1,2:T(8,128)S(1)} %copy.34), channel_id=1, source_target_pairs={{0,1},{1,2},{2,3},{3,4},{4,5},{5,6},{6,7},{8,9},{9,10},{10,11},{11... | collective-permute-start | bytes 24584 | tf_op jit(solution)/shard_map/ppermute | solution.py:16
  177.9 8.3 %collective-permute-start.22 = (f32[128,16,1]{0,1,2:T(8,128)S(1)}, f32[128,16,1]{0,1,2:T(8,128)S(1)}, u32[]{:S(2)}, u32[]{:S(2)}) collective-permute-start(f32[128,16,1]{0,1,2:T(8,128)S(1)} %copy.32), channel_id=1, source_target_pairs={{1,0},{2,1},{3,2},{4,3},{5,4},{6,5},{7,6},{9,8},{10,9},{11,10},{12... | collective-permute-start | bytes 24584 | tf_op jit(solution)/shard_map/ppermute | solution.py:19
  186.9 2.3 copy-start
  187.9 1.0 copy-start.1
  187.9 1.3 copy-start.2
  192.5 553.4 %all-reduce.5.cloned.1.call-start = ((), (), s32[]{:S(2)}) async-start(), calls=%async_computation.1 | async-start | bytes 131072 | tf_op jit(solution)/shard_map/psum | solution.py:66
Sparse Core Ops, SparseCore 0:
  192.6 264.7 all-reduce.2
  490.4 255.3 all-reduce.4
where the time goes:
time: 800 us; the launch traced here: 785 us
  waiting for transfers between devices  557 us (70%)
  starting transfers between devices  111 us (14%)
  other arithmetic  62.8 us (8%)
  local copies, waits for them, and re-layouts  22 us (3%)
  matrix products  16.9 us (2%)
  between operations  14.8 us (2%)
    psum x2, waiting for transfers between devices, orthonormalize(): gram = lax.psum(local_gram, ('lon', 'lat'))  516 us
    ppermute x12, starting transfers between devices, extended(): lax.ppermute(lax.slice_in_dim(block, 0, width, axis=dim), axis, backward)  62.9 us
    ppermute x12, starting transfers between devices, extended(): lax.ppermute(lax.slice_in_dim(block, block.shape[dim] - width, None, axis...  48.4 us
    ppermute x12, waiting for transfers between devices, extended(): lax.ppermute(lax.slice_in_dim(block, 0, width, axis=dim), axis, backward)  41.4 us
    another operation x6, other arithmetic, orthonormalize(): lower = jnp.linalg.cholesky(gram)  25 us
    another operation x4, other arithmetic, orthonormalize(): inverse = jax.scipy.linalg.solve_triangular(lower, eye, lower=True)  20.9 us
  transfers between devices with their start and end apart: 26, of which 13 were waited for; matrix products, arithmetic and copies ran while one was open for 2% of the time, Pallas kernels for 0%

commit v1 on v0

v1 whole, which is shorter than its diff:
```python
import functools

import jax
import jax.numpy as jnp
from jax import lax
from jax.experimental import pallas as pl
from jax.experimental.pallas import tpu as pltpu
from jax.sharding import PartitionSpec as P

PASSES = 4
MARGIN = PASSES + 1
CORES = 2
Y_LOW = 4
Y_HIGH = 2
MESH = pl.DeviceIdType.MESH
HIGHEST = lax.Precision.HIGHEST


class Place:
    def __init__(self, n_lon, n_lat):
        self.n_lon, self.n_lat = n_lon, n_lat
        self.n_z = n_lon // (Y_LOW * CORES)
        self.n_x = n_lat // Y_HIGH
        self.size_a = self.n_z * CORES
        self.size_b = n_lat * Y_LOW
        self.lon = lax.axis_index("lon")
        self.lat = lax.axis_index("lat")
        core = lax.rem(self.lon, CORES)
        pair = lax.div(self.lon, CORES)
        y_low = lax.rem(pair, Y_LOW)
        z = lax.div(pair, Y_LOW)
        self.core, self.y_low, self.z = core, y_low, z
        self.rank_a = z * CORES + core
        self.rank_b = self.lat * Y_LOW + y_low

    def peer_a(self, step):
        rank = lax.rem(self.rank_a + step, self.size_a)
        lon = (lax.div(rank, CORES) * Y_LOW + self.y_low) * CORES + lax.rem(rank, CORES)
        return rank, (lon, self.lat)

    def peer_b(self, step):
        rank = lax.rem(self.rank_b + step, self.size_b)
        lon = (self.z * Y_LOW + lax.rem(rank, Y_LOW)) * CORES + self.core
        return rank, (lon, lax.div(rank, Y_LOW))

    def near(self, dlon, dlat):
        return (
            lax.rem(self.lon + dlon + self.n_lon, self.n_lon),
            lax.rem(self.lat + dlat + self.n_lat, self.n_lat),
        )


def greet(place, others):
    barrier = pltpu.get_barrier_semaphore()
    for device in others:
        pl.semaphore_signal(barrier, inc=1, device_id=device, device_id_type=MESH)

    def greet_a(step, _):
        pl.semaphore_signal(barrier, inc=1, device_id=place.peer_a(step)[1], device_id_type=MESH)
        return 0

    def greet_b(step, _):
        pl.semaphore_signal(barrier, inc=1, device_id=place.peer_b(step)[1], device_id_type=MESH)
        return 0

    lax.fori_loop(1, place.size_a, greet_a, 0)
    lax.fori_loop(1, place.size_b, greet_b, 0)
    return len(others) + place.size_a + place.size_b - 2


def all_reduce(place, part, slots_a, slots_b, total, sems):
    send_a, recv_a, send_b, recv_b, send_c, recv_c = sems
    mine = place.rank_a

    def copy_a(step, recv_rank):
        rank, device = place.peer_a(step)
        return pltpu.make_async_remote_copy(
            src_ref=part.at[rank],
            dst_ref=slots_a.at[mine],
            send_sem=send_a.at[rank],
            recv_sem=recv_a.at[recv_rank],
            device_id=device,
            device_id_type=MESH,
        )

    def copy_b(step, recv_rank):
        rank, device = place.peer_b(step)
        return pltpu.make_async_remote_copy(
            src_ref=slots_b.at[place.rank_b],
            dst_ref=slots_b.at[place.rank_b],
            send_sem=send_b.at[rank],
            recv_sem=recv_b.at[recv_rank],
            device_id=device,
            device_id_type=MESH,
        )

    def copy_c(step, recv_rank):
        rank, device = place.peer_a(step)
        return pltpu.make_async_remote_copy(
            src_ref=total.at[mine],
            dst_ref=total.at[mine],
            send_sem=send_c.at[rank],
            recv_sem=recv_c.at[recv_rank],
            device_id=device,
            device_id_type=MESH,
        )

    def start(copy, rank, size):
        def body(step, _):
            copy(step, rank).start()
            return 0

        lax.fori_loop(1, size, body, 0)

    def finish(copy, peer, size):
        def body(step, _):
            rank, _ = peer(step)
            copy(step, rank).wait_recv()
            return 0

        lax.fori_loop(1, size, body, 0)

    def drain(copy, rank, size):
        def body(step, _):
            copy(step, rank).wait_send()
            return 0

        lax.fori_loop(1, size, body, 0)

    start(copy_a, mine, place.size_a)
    slots_a[mine] = part[mine]
    finish(copy_a, place.peer_a, place.size_a)
    slots_b[place.rank_b] = jnp.sum(slots_a[...], axis=0)
    start(copy_b, place.rank_b, place.size_b)
    finish(copy_b, place.peer_b, place.size_b)
    total[mine] = jnp.sum(slots_b[...], axis=0)
    start(copy_c, mine, place.size_a)
    finish(copy_c, place.peer_a, place.size_a)
    drain(copy_a, mine, place.size_a)
    drain(copy_b, place.rank_b, place.size_b)
    drain(copy_c, mine, place.size_a)


def reduce_scratch(size_a, size_b, snaps):
    rows = snaps // size_a
    return [
        pltpu.VMEM((size_a, rows, snaps), jnp.float32),
        pltpu.VMEM((size_a, rows, snaps), jnp.float32),
        pltpu.VMEM((size_b, rows, snaps), jnp.float32),
        pltpu.SemaphoreType.DMA((size_a,)),
        pltpu.SemaphoreType.DMA((size_a,)),
        pltpu.SemaphoreType.DMA((size_b,)),
        pltpu.SemaphoreType.DMA((size_b,)),
        pltpu.SemaphoreType.DMA((size_a,)),
        pltpu.SemaphoreType.DMA((size_a,)),
    ]


NEIGHBOURS = [(a, b) for a in (-1, 0, 1) for b in (-1, 0, 1) if (a, b) != (0, 0)]


def first_kernel(
    n_lon, n_lat,
    p_ref, mask_ref, flat_ref, gram_ref,
    raw, wide_mask, even, odd, quarter, keep_lon, keep_lat, halves, flat,
    part, slots_a, slots_b, sa, ra, sb, rb, sc, rc,
    send_near, recv_near, send_mask, recv_mask, out_sem,
):
    place = Place(n_lon, n_lat)
    clon, clat = mask_ref.shape
    snaps = raw.shape[2]
    base = 8
    wide = clat + 2 * base
    rows = clon + 2 * MARGIN
    expected = greet(place, [place.near(a, b) for a, b in NEIGHBOURS])

    lon0, lat0 = 8, clat
    wide_mask[lon0 : lon0 + clon, lat0 : lat0 + clat] = mask_ref[...].astype(jnp.float32)

    def turn(row):
        raw[MARGIN + row, base : base + clat, :] = p_ref[pl.ds(row, snaps, stride=clon), :].T

    edge = sorted(set(range(MARGIN)) | set(range(clon - MARGIN, clon)))
    for row in edge:
        turn(row)
    for row in range(clon):
        if row not in edge:
            turn(row)

    pl.semaphore_wait(pltpu.get_barrier_semaphore(), expected)

    def span(delta, own_at, own, margin):
        if delta == 0:
            return pl.ds(own_at, own), pl.ds(own_at, own)
        if delta > 0:
            return pl.ds(own_at + own - margin, margin), pl.ds(own_at - margin, margin)
        return pl.ds(own_at, margin), pl.ds(own_at + own, margin)

    copies = []
    for index, (a, b) in enumerate(NEIGHBOURS):
        src_lon, dst_lon = span(a, MARGIN, clon, MARGIN)
        src_lat, dst_lat = span(b, base, clat, base)
        copies.append(
            pltpu.make_async_remote_copy(
                src_ref=raw.at[src_lon, src_lat, :],
                dst_ref=raw.at[dst_lon, dst_lat, :],
                send_sem=send_near.at[index],
                recv_sem=recv_near.at[index],
                device_id=place.near(a, b),
                device_id_type=MESH,
            )
        )
        src_lon, dst_lon = span(a, lon0, clon, 8)
        src_lat, dst_lat = span(b, lat0, clat, clat)
        copies.append(
            pltpu.make_async_remote_copy(
                src_ref=wide_mask.at[src_lon, src_lat],
                dst_ref=wide_mask.at[dst_lon, dst_lat],
                send_sem=send_mask.at[index],
                recv_sem=recv_mask.at[index],
                device_id=place.near(a, b),
                device_id_type=MESH,
            )
        )
    for copy in copies:
        copy.start()
    for copy in copies:
        copy.wait_recv()

    low = jnp.where(place.lat > 0, 1.0, 0.0)
    high = jnp.where(place.lat < n_lat - 1, 1.0, 0.0)
    turned = jnp.concatenate(
        [
            wide_mask[:, 0:clat].T[clat - base :, :] * low,
            wide_mask[:, clat : 2 * clat].T,
            wide_mask[:, 2 * clat :].T[:base, :] * high,
        ],
        axis=0,
    )
    skip = lon0 - MARGIN
    for row in range(rows):
        quarter[row] = 0.25 * jnp.broadcast_to(turned[:, row + skip : row + skip + 1], (wide, snaps))

    def coefficients(row, _):
        own = quarter[row]
        keep_lat[row] = 1.0 - (pltpu.roll(own, 1, 0) + pltpu.roll(own, wide - 1, 0))
        even[row] = raw[row] * (4.0 * own)
        return 0

    def coefficients_lon(row, _):
        keep_lon[row] = 1.0 - (quarter[row - 1] + quarter[row + 1])
        return 0

    lax.fori_loop(0, rows, coefficients, 0)
    lax.fori_loop(1, rows - 1, coefficients_lon, 0)

    def sweep(source, target, row):
        scale = quarter[row]
        lon_swept = source[row] * keep_lon[row] + scale * (source[row - 1] + source[row + 1])
        sides = pltpu.roll(lon_swept, 1, 0) + pltpu.roll(lon_swept, wide - 1, 0)
        target[row] = lon_swept * keep_lat[row] + scale * sides

    for step in range(PASSES):
        source, target = (even, odd) if step % 2 == 0 else (odd, even)

        def one_row(row, _, source=source, target=target):
            sweep(source, target, row)
            return 0

        lax.fori_loop(1 + step, rows - 1 - step, one_row, 0)
    field = even if PASSES % 2 == 0 else odd

    def gradients(row, _):
        at = row + MARGIN
        half = 2.0 * quarter[at]
        centre = field[at]
        own = slice(base, base + clat)
        flat[0, row] = centre[own]
        flat[1, row] = (half * (field[at + 1] - field[at - 1]))[own]
        flat[2, row] = (half * (pltpu.roll(centre, wide - 1, 0) - pltpu.roll(centre, 1, 0)))[own]
        return 0

    lax.fori_loop(0, clon, gradients, 0)
    out = pltpu.make_async_copy(flat, flat_ref, out_sem)
    out.start()

    group = 8
    chunks = 3 * clon // group
    per = clon // group

    def gram_chunk(index, total):
        block = flat[lax.div(index, per), pl.ds(lax.rem(index, per) * group, group)]
        block = block.reshape(group * clat, snaps)
        return total + lax.dot_general(
            block, block, (((0,), (0,)), ((), ())), precision=HIGHEST, preferred_element_type=jnp.float32
        )

    gram = lax.fori_loop(0, chunks, gram_chunk, jnp.zeros((snaps, snaps), jnp.float32))
    part[...] = gram.reshape(part.shape)
    all_reduce(place, part, slots_a, slots_b, gram_ref, (sa, ra, sb, rb, sc, rc))
    for copy in copies:
        copy.wait_send()
    out.wait()


def second_kernel(
    n_lon, n_lat,
    flat_ref, inverse_ref, basis_ref, gram_ref,
    basis, part, slots_a, slots_b, sa, ra, sb, rb, sc, rc, out_sem,
):
    place = Place(n_lon, n_lat)
    expected = greet(place, [])
    _, clon, clat, snaps = flat_ref.shape
    group = 8
    chunks = 3 * clon // group
    per = clon // group

    def chunk(index, total):
        which, where = lax.div(index, per), lax.rem(index, per) * group
        block = flat_ref[which, pl.ds(where, group)].reshape(group * clat, snaps)
        turned = lax.dot_general(
            block,
            inverse_ref[...],
            (((1,), (1,)), ((), ())),
            precision=HIGHEST,
            preferred_element_type=jnp.float32,
        )
        basis[which, pl.ds(where, group)] = turned.reshape(group, clat, snaps)
        return total + lax.dot_general(
            turned, turned, (((0,), (0,)), ((), ())), precision=HIGHEST, preferred_element_type=jnp.float32
        )

    gram = lax.fori_loop(0, chunks, chunk, jnp.zeros((snaps, snaps), jnp.float32))
    out = pltpu.make_async_copy(basis, basis_ref, out_sem)
    out.start()
    part[...] = gram.reshape(part.shape)
    pl.semaphore_wait(pltpu.get_barrier_semaphore(), expected)
    all_reduce(place, part, slots_a, slots_b, gram_ref, (sa, ra, sb, rb, sc, rc))
    out.wait()


def last_kernel(scale, basis_ref, inverse_ref, modes_ref):
    _, clon, clat, snaps = basis_ref.shape
    inverse = inverse_ref[...]

    def one(row, _):
        value = lax.dot_general(
            inverse,
            basis_ref[0, row],
            (((1,), (1,)), ((), ())),
            precision=HIGHEST,
            preferred_element_type=jnp.float32,
        )
        modes_ref[:, 0, row, :] = value * scale
        return 0

    lax.fori_loop(0, clon, one, 0, unroll=4)


def whole(memory_space=pltpu.VMEM):
    return pl.BlockSpec(memory_space=memory_space)


def factor(gram):
    lower = jnp.linalg.cholesky(gram)
    eye = jnp.eye(gram.shape[0], dtype=jnp.float32)
    return lower, jax.scipy.linalg.solve_triangular(lower, eye, lower=True)


def on_device(n_lon, n_lat, pressure, ocean_mask):
    snaps, clon, clat = pressure.shape
    size_a = n_lon // Y_LOW
    size_b = n_lat * Y_LOW
    wide, rows = clat + 16, clon + 2 * MARGIN
    f32 = jnp.float32
    limit = 56 * 1024 * 1024
    extended = [pltpu.VMEM((rows, wide, snaps), f32)]
    flat_shape = (3, clon, clat, snaps)
    gram_shape = (size_a, snaps // size_a, snaps)
    flat, gram = pl.pallas_call(
        functools.partial(first_kernel, n_lon, n_lat),
        out_shape=(jax.ShapeDtypeStruct(flat_shape, f32), jax.ShapeDtypeStruct(gram_shape, f32)),
        in_specs=[whole(), whole()],
        out_specs=(whole(pl.ANY), whole()),
        scratch_shapes=extended
        + [pltpu.VMEM((clon + 16, 3 * clat), f32)]
        + 5 * extended
        + [pltpu.VMEM((8, 128), f32), pltpu.VMEM(flat_shape, f32)]
        + reduce_scratch(size_a, size_b, snaps)
        + 4 * [pltpu.SemaphoreType.DMA((len(NEIGHBOURS),))]
        + [pltpu.SemaphoreType.DMA],
        compiler_params=pltpu.CompilerParams(
            collective_id=0, has_side_effects=True, vmem_limit_bytes=limit
        ),
        name="filter_gram",
    )(pressure.reshape(snaps * clon, clat), ocean_mask)
    lower_one, inverse_one = factor(gram.reshape(snaps, snaps))
    basis, gram = pl.pallas_call(
        functools.partial(second_kernel, n_lon, n_lat),
        out_shape=(jax.ShapeDtypeStruct(flat_shape, f32), jax.ShapeDtypeStruct(gram_shape, f32)),
        in_specs=[whole(), whole()],
        out_specs=(whole(pl.ANY), whole()),
        scratch_shapes=[pltpu.VMEM(flat_shape, f32)]
        + reduce_scratch(size_a, size_b, snaps)
        + [pltpu.SemaphoreType.DMA],
        compiler_params=pltpu.CompilerParams(
            collective_id=1, has_side_effects=True, vmem_limit_bytes=limit
        ),
        name="basis_gram",
    )(flat, inverse_one)
    lower_two, inverse_two = factor(gram.reshape(snaps, snaps))
    total_rows = 3 * clon * clat * n_lon * n_lat
    scale = float(total_rows) ** 0.5
    modes = pl.pallas_call(
        functools.partial(last_kernel, scale),
        grid=(3,),
        out_shape=jax.ShapeDtypeStruct((snaps, 3, clon, clat), f32),
        in_specs=[pl.BlockSpec((1, clon, clat, snaps), lambda i: (i, 0, 0, 0)), whole()],
        out_specs=pl.BlockSpec((snaps, 1, clon, clat), lambda i: (0, i, 0, 0)),
        compiler_params=pltpu.CompilerParams(vmem_limit_bytes=32 * 1024 * 1024),
        name="modes",
    )(basis, inverse_two)
    factor_r = (
        jnp.dot(lower_two.T, lower_one.T, precision=HIGHEST, preferred_element_type=f32) / scale
    )
    return (modes, factor_r)


def solution(mesh):
    n_lon, n_lat = mesh.shape["lon"], mesh.shape["lat"]
    return jax.shard_map(
        functools.partial(on_device, n_lon, n_lat),
        mesh=mesh,
        in_specs=(P(None, "lon", "lat"), P("lon", "lat")),
        out_specs=(P(None, None, "lon", "lat"), P()),
        check_vma=False,
    )
```

time: 800 us -> 167 us (0.21); the launches traced: 785 us -> 166 us
  waiting for transfers between devices: 557 us -> 0 us
  Pallas kernels: 0 us -> 111 us
  starting transfers between devices: 111 us -> 0 us
  local copies, waits for them, and re-layouts: 22 us -> 3.74 us
  other arithmetic: 62.8 us -> 47.3 us
  between operations: 14.8 us -> 0.72 us
  matrix products: 16.9 us -> 3.31 us
    psum x2 -> x0, waiting for transfers between devices: 516 us -> none  [orthonormalize(): gram = lax.psum(local_gram, ('lon', 'lat'))]
    ppermute x24 -> x0, starting transfers between devices: 111 us -> none  [the longest x12 62.9 us: extended(): lax.ppermute(lax.slice_in_dim(block, 0, width, axis=dim), axis, backward)]
    pallas_call x0 -> x3, Pallas kernels: none -> 111 us  [the longest x1 66.2 us: on_device(): pl.pallas_call(functools.partial(first_kernel, n_lon, n_lat), out_shape=(...]
    ppermute x24 -> x0, waiting for transfers between devices: 41.4 us -> none  [the longest x12 41.4 us: extended(): lax.ppermute(lax.slice_in_dim(block, 0, width, axis=dim), axis, backward)]
    dot_general x5 -> x1, matrix products: 16.3 us -> 2.11 us  [on_device(): jnp.dot(lower_two.T, lower_one.T, precision=HIGHEST, preferred_element_ty...]
    slice x22 -> x0, local copies, waits for them, and re-layouts: 9.69 us -> none  [the longest x15 5.13 us: extended(): lax.slice_in_dim(block, block.shape[dim] - width, None, axis=dim)]
    another operation x13 -> x10, other arithmetic: 52 us -> 45.6 us  [the longest x6 24.7 us: factor(): lower = jnp.linalg.cholesky(gram)]
  transfers between devices with their start and end apart: 26 -> 0, of which waited for: 13 -> 0; matrix products, arithmetic and copies ran while one was open for 2% -> 0% of each run, Pallas kernels for 0% -> 0%
where the time goes in v1:
time: 167 us; the launch traced here: 166 us
  Pallas kernels  111 us (66%)
  other arithmetic  47.3 us (28%)
  local copies, waits for them, and re-layouts  3.74 us (2%)
  matrix products  3.31 us (2%)
    pallas_call x1, Pallas kernels, on_device(): pl.pallas_call(functools.partial(first_kernel, n_lon, n_lat), out_shape=(...  66.2 us
    pallas_call x1, Pallas kernels, on_device(): pl.pallas_call(functools.partial(second_kernel, n_lon, n_lat), out_shape=...  35.3 us
    another operation x6, other arithmetic, factor(): lower = jnp.linalg.cholesky(gram)  24.7 us
    another operation x4, other arithmetic, factor(): return (lower, jax.scipy.linalg.solve_triangular(lower, eye, lower=True))  20.8 us
    pallas_call x1, Pallas kernels, on_device(): pl.pallas_call(functools.partial(last_kernel, scale), grid=(3,), out_shap...  9.71 us

profile of v1, /device:TPU:1, one launch (start us, length us, event | category | flops | bytes accessed | tf_op | source)
XLA Modules:
  0.0 166.2 jit_solution(1318545439974253961)
XLA Ops:
  0.6 66.2 %filter_gram.1 = (f32[3,16,128,128]{3,2,1,0:T(8,128)}, f32[16,8,128]{2,1,0:T(8,128)}) custom-call(f32[2048,128]{1,0:T(8,128)} %bitcast.23, s32[16,128]{1,0:T(8,128)} %mask_ref.1), custom_call_target="tpu_custom_call" | custom-call | tf_op jit(solution)/shard_map/filter_gram/pallas_call | solution.py:380
  66.8 0.9 copy.8
  67.7 0.9 fusion.7
  68.6 11.7 %cholesky.44 = f32[128,128]{1,0:T(8,128)S(1)} custom-call(f32[128,128]{1,0:T(8,128)S(1)} %fusion.7), custom_call_target="Cholesky" | custom-call | tf_op jit(solution)/shard_map/jit(cholesky)/cholesky | solution.py:365
  80.3 0.6 compare_reduce_fusion.1
  81.0 0.7 select_bitcast_fusion.1
  81.6 9.8 %custom-call.6 = f32[1,128,128]{1,2,0:T(8,128)S(1)} custom-call(f32[1,128,128]{2,1,0:T(8,128)S(1)} %select_bitcast_fusion.1), custom_call_target="InvertDiagBlocksLowerTriangular" | custom-call | tf_op jit(solution)/shard_map/jit(_solve_triangular)/triangular_solve | solution.py:367
  91.5 0.9 fusion.2.inverse_ref
  92.4 35.3 %basis_gram.1 = (f32[3,16,128,128]{3,2,1,0:T(8,128)}, f32[16,8,128]{2,1,0:T(8,128)}) custom-call(f32[3,16,128,128]{3,2,1,0:T(8,128)} %get-tuple-element.8.flat_ref, f32[128,128]{1,0:T(8,128)} %fusion.2.inverse_ref), custom_call_target="tpu_custom_call" | custom-call | tf_op jit(solution)/shard_map/basis_gram/pallas_call | solution.py:398
  127.6 0.9 copy.9
  128.6 0.9 fusion.5
  129.4 11.7 %cholesky.55 = f32[128,128]{1,0:T(8,128)S(1)} custom-call(f32[128,128]{1,0:T(8,128)S(1)} %fusion.5), custom_call_target="Cholesky" | custom-call | tf_op jit(solution)/shard_map/jit(cholesky)/cholesky | solution.py:365
  141.2 0.6 compare_reduce_fusion
  141.8 2.1 %convolution_multiply_fusion = f32[128,128]{1,0:T(8,128)} fusion(f32[128,128]{1,0:T(8,128)S(1)} %cholesky.44, f32[128,128]{1,0:T(8,128)S(1)} %cholesky.55, pred[]{:T(512)} %compare_reduce_fusion, pred[]{:T(512)} %compare_reduce_fusion.1), kind=kOutput, calls=%fused_computation | convolution fusion | flops 25280512 | bytes 196610 | tf_op jit(solution)/shard_map/dot_general | solution.py:424
  143.9 0.6 select_bitcast_fusion
  144.5 9.8 %custom-call.7 = f32[1,128,128]{1,2,0:T(8,128)S(1)} custom-call(f32[1,128,128]{2,1,0:T(8,128)S(1)} %select_bitcast_fusion), custom_call_target="InvertDiagBlocksLowerTriangular" | custom-call | tf_op jit(solution)/shard_map/jit(_solve_triangular)/triangular_solve | solution.py:367
  154.3 0.3 fusion.inverse_ref
  154.6 0.0 copy-start
  154.6 1.9 %copy-done = f32[3,16,128,128]{3,2,1,0:T(8,128)S(1)} copy-done((f32[3,16,128,128]{3,2,1,0:T(8,128)S(1)}, f32[3,16,128,128]{3,2,1,0:T(8,128)}, u32[]{:S(2)}) %copy-start) | copy-done | bytes 3145752
  156.5 9.7 %modes.1 = f32[128,3,16,128]{3,2,1,0:T(8,128)} custom-call(f32[3,16,128,128]{3,2,1,0:T(8,128)S(1)} %copy-done, f32[128,128]{1,0:T(8,128)S(1)} %fusion.inverse_ref), custom_call_target="tpu_custom_call" | custom-call | tf_op jit(solution)/shard_map/modes/pallas_call | solution.py:414
  (2 shorter events, 0.1 us)
Async XLA Ops:
  154.6 1.9 %copy-start = (f32[3,16,128,128]{3,2,1,0:T(8,128)S(1)}, f32[3,16,128,128]{3,2,1,0:T(8,128)}, u32[]{:S(2)}) copy-start(f32[3,16,128,128]{3,2,1,0:T(8,128)} %get-tuple-element.10.basis_ref) | copy-start | bytes 9437188

commit v2 on v0

v2 whole, which is shorter than its diff:
```python
import functools

import jax
import jax.numpy as jnp
from jax import lax
from jax.experimental import pallas as pl
from jax.experimental.pallas import tpu as pltpu
from jax.sharding import PartitionSpec as P

PASSES = 4
MARGIN = PASSES + 1
CORES = 2
Y_LOW = 4
Y_HIGH = 2
BLOCK = 16
BASE = 8
MESH = pl.DeviceIdType.MESH
HIGHEST = lax.Precision.HIGHEST
F32, BF16 = jnp.float32, jnp.bfloat16


def steps_of(size):
    return sorted(range(1, size), key=lambda step: -min(step, size - step))


class Place:
    def __init__(self, n_lon, n_lat):
        self.n_lon, self.n_lat = n_lon, n_lat
        self.n_z = n_lon // (Y_LOW * CORES)
        self.n_y = Y_LOW * Y_HIGH
        self.n_x = n_lat // Y_HIGH
        self.n_a = self.n_x * CORES
        self.lon = lax.axis_index("lon")
        self.lat = lax.axis_index("lat")
        pair = lax.div(self.lon, CORES)
        self.core = lax.rem(self.lon, CORES)
        self.z = lax.div(pair, Y_LOW)
        self.x = lax.div(self.lat, Y_HIGH)
        self.y = lax.rem(self.lat, Y_HIGH) * Y_LOW + lax.rem(pair, Y_LOW)
        self.a = self.x * CORES + self.core

    def device(self, x, y, z, core):
        lon = (z * Y_LOW + lax.rem(y, Y_LOW)) * CORES + core
        return lon, x * Y_HIGH + lax.div(y, Y_LOW)

    def peer_a(self, step):
        rank = lax.rem(self.a + step, self.n_a)
        return rank, self.device(lax.div(rank, CORES), self.y, self.z, lax.rem(rank, CORES))

    def peer_y(self, step):
        rank = lax.rem(self.y + step, self.n_y)
        return rank, self.device(self.x, rank, self.z, self.core)

    def peer_z(self, step):
        rank = lax.rem(self.z + step, self.n_z)
        return rank, self.device(self.x, self.y, rank, self.core)

    def near(self, dlon, dlat):
        return (
            lax.rem(self.lon + dlon + self.n_lon, self.n_lon),
            lax.rem(self.lat + dlat + self.n_lat, self.n_lat),
        )

    def reduce_peers(self):
        groups = ((self.peer_a, self.n_a), (self.peer_y, self.n_y), (self.peer_z, self.n_z))
        return [peer(step)[1] for peer, size in groups for step in steps_of(size)]


def greet(devices):
    barrier = pltpu.get_barrier_semaphore()
    for device in devices:
        pl.semaphore_signal(barrier, inc=1, device_id=device, device_id_type=MESH)
    return len(devices)


def send(src, dst, send_sem, recv_sem, device):
    return pltpu.make_async_remote_copy(
        src_ref=src,
        dst_ref=dst,
        send_sem=send_sem,
        recv_sem=recv_sem,
        device_id=device,
        device_id_type=MESH,
    )


def exchange(peer, size, mine, source, target, sends, recvs):
    ranks = [peer(step) for step in steps_of(size)]
    started = [
        send(source(rank), target.at[mine], sends.at[rank], recvs.at[mine], device)
        for rank, device in ranks
    ]
    for copy in started:
        copy.start()

    def arrived():
        for rank, device in ranks:
            send(source(rank), target.at[rank], sends.at[rank], recvs.at[rank], device).wait_recv()

    def sent():
        for copy in started:
            copy.wait_send()

    return arrived, sent


def all_reduce(place, part, slots_a, slots_y, slots_z, total, sems):
    a, y, z = place.a, place.y, place.z
    arrived, sent_a = exchange(
        place.peer_a, place.n_a, a, lambda rank: part.at[rank], slots_a, sems[0], sems[1]
    )
    slots_a[a] = part[a]
    arrived()
    slots_y[y] = jnp.sum(slots_a[...], axis=0)
    arrived, sent_y = exchange(
        place.peer_y, place.n_y, y, lambda _: slots_y.at[y], slots_y, sems[2], sems[3]
    )
    arrived()
    slots_z[z] = jnp.sum(slots_y[...], axis=0)
    arrived, sent_z = exchange(
        place.peer_z, place.n_z, z, lambda _: slots_z.at[z], slots_z, sems[4], sems[5]
    )
    arrived()
    total[a] = jnp.sum(slots_z[...], axis=0)
    arrived, sent_b = exchange(
        place.peer_a, place.n_a, a, lambda _: total.at[a], total, sems[6], sems[7]
    )
    arrived()
    for sent in (sent_a, sent_y, sent_z, sent_b):
        sent()


def group_sizes(n_lon, n_lat):
    return n_lat // Y_HIGH * CORES, Y_LOW * Y_HIGH, n_lon // (Y_LOW * CORES)


def reduce_scratch(n_lon, n_lat, snaps):
    n_a, n_y, n_z = group_sizes(n_lon, n_lat)
    piece = (snaps // n_a, snaps)
    slots = [pltpu.VMEM((size, *piece), F32) for size in (n_a, n_a, n_y, n_z)]
    return slots + [pltpu.SemaphoreType.DMA((size,)) for size in (n_a, n_y, n_z, n_a) for _ in (0, 1)]


def split(value):
    one = value.astype(BF16)
    rest = value - one.astype(F32)
    two = rest.astype(BF16)
    return one, two, (rest - two.astype(F32)).astype(BF16)


def multiply(left, right, left_dim, right_dim):
    return lax.dot_general(
        left, right, (((left_dim,), (right_dim,)), ((), ())), preferred_element_type=F32
    )


def exact_dot(left, right, left_dim, right_dim):
    return lax.dot_general(
        left,
        right,
        (((left_dim,), (right_dim,)), ((), ())),
        precision=HIGHEST,
        preferred_element_type=F32,
    )


def set_weights(matrix, wide, narrow):
    one, two, three = split(matrix)
    pair = jnp.concatenate([one, two], axis=1)
    wide[...] = jnp.concatenate([pair, pair], axis=0)
    narrow[...] = jnp.concatenate([three, one], axis=0)


def apply_weights(value, wide, narrow):
    columns = value.shape[1]
    one, two, three = split(value)
    main = multiply(jnp.concatenate([one, two], axis=1), wide[...], 1, 0)
    rest = multiply(jnp.concatenate([one, three], axis=1), narrow[...], 1, 0)
    return main[:, :columns] + (main[:, columns:] + rest)


def gram_parts(value):
    one, two, three = split(value)
    pair = jnp.concatenate([one, two], axis=1)
    return multiply(pair, pair, 0, 0), multiply(one, three, 0, 0)


def gram_start(columns):
    return jnp.zeros((2 * columns, 2 * columns), F32), jnp.zeros((columns, columns), F32)


def gram_end(main, side):
    n = side.shape[0]
    cross = main[n:, :n] + main[:n, n:] + (main[n:, n:] + (side + side.T))
    return main[:n, :n] + cross


def span(delta, own_at, own, margin):
    if delta == 0:
        return pl.ds(own_at, own), pl.ds(own_at, own)
    if delta > 0:
        return pl.ds(own_at + own - margin, margin), pl.ds(own_at - margin, margin)
    return pl.ds(own_at, margin), pl.ds(own_at + own, margin)


def first_kernel(
    n_lon, n_lat,
    p_hbm, mask_ref, flat, gram_ref,
    p_ref, raw, masks, even, odd, quarter, keep_lon, keep_lat,
    part, slots_a, slots_y, slots_z, *sems,
):
    reduce_sems, (near_send, near_recv, load_sem) = sems[:8], sems[8:]
    place = Place(n_lon, n_lat)
    clon, clat = mask_ref.shape
    snaps = raw.shape[2]
    wide = clat + 2 * BASE
    rows = clon + 2 * MARGIN
    load = pltpu.make_async_copy(p_hbm, p_ref, load_sem)
    load.start()
    sides = [place.near(0, 1), place.near(0, -1), place.near(1, 0), place.near(-1, 0)]
    expected = greet(sides + place.reduce_peers())

    own_lon, own_lat = pl.ds(BASE, clon), pl.ds(clat, clat)
    masks[own_lon, own_lat] = mask_ref[...].astype(F32)
    load.wait()

    def turn(row):
        raw[MARGIN + row, BASE : BASE + clat, :] = p_ref[pl.ds(row, snaps, stride=clon), :].T

    for row in range(clon):
        turn(row)

    pl.semaphore_wait(pltpu.get_barrier_semaphore(), expected)

    def near(index, source, target, device):
        return send(source, target, near_send.at[index], near_recv.at[index], device)

    lat_mask, lat_field, lon_mask, lon_field, corners = [], [], [], [], []
    for index, delta in enumerate((1, -1)):
        device = place.near(0, delta)
        src, dst = span(delta, clat, clat, clat)
        lat_mask.append(
            near(index, masks.at[own_lon, own_lat], masks.at[own_lon, dst], device)
        )
        src, dst = span(delta, BASE, clat, MARGIN)
        inner = pl.ds(MARGIN, clon)
        lat_field.append(near(2 + index, raw.at[inner, src, :], raw.at[inner, dst, :], device))
    for index, delta in enumerate((1, -1)):
        device = place.near(delta, 0)
        src, dst = span(delta, BASE, clon, MARGIN)
        lon_mask.append(near(4 + index, masks.at[src, :], masks.at[dst, :], device))
        src, dst = span(delta, MARGIN, clon, MARGIN)
        inner = pl.ds(BASE, clat)
        lon_field.append(near(6 + index, raw.at[src, inner, :], raw.at[dst, inner, :], device))
        for end, at in enumerate((BASE - MARGIN, BASE + clat)):
            outer = pl.ds(at, MARGIN)
            number = 8 + 2 * index + end
            corners.append(near(number, raw.at[src, outer, :], raw.at[dst, outer, :], device))
    for copy in lat_mask + lat_field + lon_field:
        copy.start()
    for copy in lat_mask:
        copy.wait_recv()
    for copy in lon_mask:
        copy.start()
    for copy in lat_field:
        copy.wait_recv()
    for copy in corners:
        copy.start()
    for copy in lon_mask:
        copy.wait_recv()

    low = jnp.where(place.lat > 0, 1.0, 0.0)
    high = jnp.where(place.lat < n_lat - 1, 1.0, 0.0)
    turned = jnp.concatenate(
        [
            masks[:, 0:clat].T[clat - BASE :, :] * low,
            masks[:, clat : 2 * clat].T,
            masks[:, 2 * clat :].T[:BASE, :] * high,
        ],
        axis=0,
    )
    skip = BASE - MARGIN
    for row in range(rows):
        quarter[row] = 0.25 * jnp.broadcast_to(turned[:, row + skip : row + skip + 1], (wide, snaps))

    def coefficients(row, _):
        own = quarter[row]
        keep_lat[row] = 1.0 - (pltpu.roll(own, 1, 0) + pltpu.roll(own, wide - 1, 0))
        keep_lon[row] = 1.0 - (quarter[row - 1] + quarter[row + 1])
        return 0

    lax.fori_loop(1, rows - 1, coefficients, 0)
    for copy in lon_field + corners:
        copy.wait_recv()

    def masked(row, _):
        even[row] = raw[row] * (4.0 * quarter[row])
        return 0

    lax.fori_loop(0, rows, masked, 0)

    def sweep(source, target, row):
        scale = quarter[row]
        lon_swept = source[row] * keep_lon[row] + scale * (source[row - 1] + source[row + 1])
        both = pltpu.roll(lon_swept, 1, 0) + pltpu.roll(lon_swept, wide - 1, 0)
        target[row] = lon_swept * keep_lat[row] + scale * both

    for step in range(PASSES):
        source, target = (even, odd) if step % 2 == 0 else (odd, even)

        def one_row(row, _, source=source, target=target):
            sweep(source, target, row)
            return 0

        lax.fori_loop(1 + step, rows - 1 - step, one_row, 0)
    field = even if PASSES % 2 == 0 else odd

    def gradients(row, _):
        at = row + MARGIN
        half = 2.0 * quarter[at]
        centre = field[at]
        own = slice(BASE, BASE + clat)
        flat[0, row] = centre[own]
        flat[1, row] = (half * (field[at + 1] - field[at - 1]))[own]
        flat[2, row] = (half * (pltpu.roll(centre, wide - 1, 0) - pltpu.roll(centre, 1, 0)))[own]
        return 0

    lax.fori_loop(0, clon, gradients, 0)

    def gram_chunk(which, carry):
        main, side = gram_parts(flat[which].reshape(clon * clat, snaps))
        return carry[0] + main, carry[1] + side

    gram = gram_end(*lax.fori_loop(0, 3, gram_chunk, gram_start(snaps)))
    part[...] = gram.reshape(part.shape)
    all_reduce(place, part, slots_a, slots_y, slots_z, gram_ref, reduce_sems)
    for copy in lat_mask + lat_field + lon_mask + lon_field + corners:
        copy.wait_send()


def second_kernel(
    n_lon, n_lat,
    flat_ref, inverse_ref, basis, gram_ref,
    wide, narrow, part, slots_a, slots_y, slots_z, *sems,
):
    place = Place(n_lon, n_lat)
    expected = greet(place.reduce_peers())
    _, clon, clat, snaps = flat_ref.shape
    group = 8
    per = clon // group
    set_weights(inverse_ref[...].T, wide, narrow)

    def chunk(index, carry):
        which, where = lax.div(index, per), lax.rem(index, per) * group
        value = flat_ref[which, pl.ds(where, group)].reshape(group * clat, snaps)
        value = apply_weights(value, wide, narrow)
        basis[which, pl.ds(where, group)] = value.reshape(group, clat, snaps)
        main, side = gram_parts(value)
        return carry[0] + main, carry[1] + side

    gram = gram_end(*lax.fori_loop(0, 3 * per, chunk, gram_start(snaps)))
    part[...] = gram.reshape(part.shape)
    pl.semaphore_wait(pltpu.get_barrier_semaphore(), expected)
    all_reduce(place, part, slots_a, slots_y, slots_z, gram_ref, sems)


def factorize(gram, left_work, right_work, panel, spread, upper_ref, inverse_ref):
    n = gram.shape[0]
    rows = lax.broadcasted_iota(jnp.int32, (n, n), 0)
    columns = lax.broadcasted_iota(jnp.int32, (n, n), 1)
    left_work[...] = gram
    right_work[...] = jnp.where(rows == columns, 1.0, 0.0)
    for at in range(0, n, BLOCK):
        for j in range(BLOCK):
            column = left_work[at : at + BLOCK, at + j : at + j + 1]
            spread[j] = jnp.broadcast_to(column, (BLOCK, n))

        def row_of(ref, i):
            return jnp.broadcast_to(ref[i : i + 1, :], (8, n))

        scalar = {
            (i, j): row_of(spread.at[j], i) for j in range(BLOCK) for i in range(j, BLOCK)
        }
        left = [row_of(left_work, at + i) for i in range(BLOCK)]
        right = [row_of(right_work, at + i) for i in range(BLOCK)]
        for j in range(BLOCK):
            pivot = scalar[j, j]
            root = lax.rsqrt(pivot)
            root = root * (1.5 - 0.5 * pivot * root * root)
            below = {i: scalar[i, j] * root for i in range(j + 1, BLOCK)}
            left[j] = left[j] * root
            right[j] = right[j] * root
            for i in range(j + 1, BLOCK):
                for k in range(j + 1, i + 1):
                    scalar[i, k] = scalar[i, k] - below[i] * below[k]
                left[i] = left[i] - below[i] * left[j]
                right[i] = right[i] - below[i] * right[j]
        for j in range(BLOCK):
            panel[j : j + 1, :n] = left[j][:1]
            panel[j : j + 1, n:] = right[j][:1]
        done = at + BLOCK
        upper_ref[at:done, :] = panel[:, :n]
        inverse_ref[at:done, :] = panel[:, n:]
        for low, high in ((done, done + BLOCK), (done + BLOCK, n)):
            if low < high <= n:
                change = exact_dot(panel[:, low:high], panel[...], 0, 0)
                left_work[low:high, :] = left_work[low:high, :] - change[:, :n]
                right_work[low:high, :] = right_work[low:high, :] - change[:, n:]
    upper_ref[...] = jnp.where(columns >= rows, upper_ref[...], 0.0)


def factor_scratch(n):
    return [
        pltpu.VMEM((n, n), F32),
        pltpu.VMEM((n, n), F32),
        pltpu.VMEM((BLOCK, 2 * n), F32),
        pltpu.VMEM((BLOCK, BLOCK, n), F32),
    ]


def factor_kernel(gram_ref, upper_ref, inverse_ref, *work):
    factorize(gram_ref[...].reshape(upper_ref.shape), *work, upper_ref, inverse_ref)


def last_kernel(
    scale,
    basis, gram_ref, first_upper, modes_ref, factor_ref,
    upper, inverse, wide, narrow, staged, out_sem, *work,
):
    _, clon, clat, snaps = basis.shape
    factorize(gram_ref[...].reshape(upper.shape), *work, upper, inverse)
    set_weights(inverse[...].T * scale, wide, narrow)
    group = 8
    copies = []
    for which in range(3):
        for part in range(clon // group):
            start = part * group
            value = basis[which, start : start + group].reshape(group * clat, snaps)
            value = apply_weights(value, wide, narrow)
            for row in range(group):
                staged[:, which, start + row, :] = value[row * clat : (row + 1) * clat].T
            here = (slice(None), which, pl.ds(start, group), slice(None))
            copy = pltpu.make_async_copy(staged.at[here], modes_ref.at[here], out_sem.at[len(copies)])
            copy.start()
            copies.append(copy)
    factor_ref[...] = exact_dot(upper[...], first_upper[...], 1, 0) * (1.0 / scale)
    for copy in copies:
        copy.wait()


def whole(memory_space=pltpu.VMEM):
    return pl.BlockSpec(memory_space=memory_space)


def on_device(n_lon, n_lat, pressure, ocean_mask):
    snaps, clon, clat = pressure.shape
    n_a, _, _ = group_sizes(n_lon, n_lat)
    rows, wide = clon + 2 * MARGIN, clat + 2 * BASE
    mib = 1024 * 1024
    flat = jax.ShapeDtypeStruct((3, clon, clat, snaps), F32)
    pieces = jax.ShapeDtypeStruct((n_a, snaps // n_a, snaps), F32)
    square = jax.ShapeDtypeStruct((snaps, snaps), F32)
    weights = [pltpu.VMEM((2 * snaps, 2 * snaps), BF16), pltpu.VMEM((2 * snaps, snaps), BF16)]
    extended = pltpu.VMEM((rows, wide, snaps), F32)

    def params(limit, collective_id=None):
        more = {} if collective_id is None else {"collective_id": collective_id, "has_side_effects": True}
        return pltpu.CompilerParams(vmem_limit_bytes=limit * mib, **more)

    field, gram = pl.pallas_call(
        functools.partial(first_kernel, n_lon, n_lat),
        out_shape=(flat, pieces),
        in_specs=[whole(pltpu.HBM), whole()],
        out_specs=(whole(), whole()),
        scratch_shapes=[pltpu.VMEM((snaps * clon, clat), F32), extended]
        + [pltpu.VMEM((clon + 2 * BASE, 3 * clat), F32)]
        + 5 * [extended]
        + reduce_scratch(n_lon, n_lat, snaps)
        + 2 * [pltpu.SemaphoreType.DMA((12,))]
        + [pltpu.SemaphoreType.DMA],
        compiler_params=params(32, 0),
        name="filter_gram",
    )(
        pltpu.with_memory_space_constraint(pressure.reshape(snaps * clon, clat), pltpu.HBM), ocean_mask
    )
    first_upper, first_inverse = pl.pallas_call(
        factor_kernel,
        out_shape=(square, square),
        in_specs=[whole()],
        out_specs=(whole(), whole()),
        scratch_shapes=factor_scratch(snaps),
        compiler_params=params(8),
        name="factor",
    )(gram)
    basis, gram = pl.pallas_call(
        functools.partial(second_kernel, n_lon, n_lat),
        out_shape=(flat, pieces),
        in_specs=[whole(), whole()],
        out_specs=(whole(), whole()),
        scratch_shapes=weights + reduce_scratch(n_lon, n_lat, snaps),
        compiler_params=params(20, 1),
        name="basis_gram",
    )(field, first_inverse)
    scale = float(3 * clon * clat * n_lon * n_lat) ** 0.5
    return pl.pallas_call(
        functools.partial(last_kernel, scale),
        out_shape=(jax.ShapeDtypeStruct((snaps, 3, clon, clat), F32), square),
        in_specs=[whole(), whole(), whole()],
        out_specs=(whole(pltpu.HBM), whole()),
        scratch_shapes=[pltpu.VMEM((snaps, snaps), F32)] * 2
        + weights
        + [pltpu.VMEM((snaps, 3, clon, clat), F32), pltpu.SemaphoreType.DMA((6,))]
        + factor_scratch(snaps),
        compiler_params=params(24),
        name="factor_modes",
    )(basis, gram, first_upper)


def solution(mesh):
    n_lon, n_lat = mesh.shape["lon"], mesh.shape["lat"]
    return jax.shard_map(
        functools.partial(on_device, n_lon, n_lat),
        mesh=mesh,
        in_specs=(P(None, "lon", "lat"), P("lon", "lat")),
        out_specs=(P(None, None, "lon", "lat"), P()),
        check_vma=False,
    )
```

time: 800 us -> 96.5 us (0.12); the launches traced: 785 us -> 96.3 us
  waiting for transfers between devices: 557 us -> 0 us
  starting transfers between devices: 111 us -> 0 us
  Pallas kernels: 0 us -> 94.8 us
  other arithmetic: 62.8 us -> 0 us
  local copies, waits for them, and re-layouts: 22 us -> 0.69 us
  matrix products: 16.9 us -> 0 us
  between operations: 14.8 us -> 0.82 us
    psum x2 -> x0, waiting for transfers between devices: 516 us -> none  [orthonormalize(): gram = lax.psum(local_gram, ('lon', 'lat'))]
    ppermute x24 -> x0, starting transfers between devices: 111 us -> none  [the longest x12 62.9 us: extended(): lax.ppermute(lax.slice_in_dim(block, 0, width, axis=dim), axis, backward)]
    pallas_call x0 -> x4, Pallas kernels: none -> 94.8 us  [the longest x1 54.3 us: on_device(): pl.pallas_call(functools.partial(first_kernel, n_lon, n_lat), out_shape=(...]
    another operation x13 -> x0, other arithmetic: 52 us -> none  [the longest x6 25 us: orthonormalize(): lower = jnp.linalg.cholesky(gram)]
    ppermute x24 -> x0, waiting for transfers between devices: 41.4 us -> none  [the longest x12 41.4 us: extended(): lax.ppermute(lax.slice_in_dim(block, 0, width, axis=dim), axis, backward)]
    dot_general x5 -> x0, matrix products: 16.3 us -> none  [the longest x2 7.65 us: orthonormalize(): jnp.dot(inverse, flat, precision=lax.Precision.HIGHEST, preferred_element...]
    slice x22 -> x0, local copies, waits for them, and re-layouts: 9.69 us -> none  [the longest x15 5.13 us: extended(): lax.slice_in_dim(block, block.shape[dim] - width, None, axis=dim)]
  transfers between devices with their start and end apart: 26 -> 0, of which waited for: 13 -> 0; matrix products, arithmetic and copies ran while one was open for 2% -> 0% of each run, Pallas kernels for 0% -> 0%
where the time goes in v2:
time: 96.5 us; the launch traced here: 96.3 us
  Pallas kernels  94.8 us (98%)
    pallas_call x1, Pallas kernels, on_device(): pl.pallas_call(functools.partial(first_kernel, n_lon, n_lat), out_shape=(...  54.3 us
    pallas_call x1, Pallas kernels, on_device(): pl.pallas_call(functools.partial(second_kernel, n_lon, n_lat), out_shape=...  23.8 us
    pallas_call x1, Pallas kernels, on_device(): pl.pallas_call(functools.partial(last_kernel, scale), out_shape=(jax.Shap...  11.1 us
    pallas_call x1, Pallas kernels, on_device(): pl.pallas_call(factor_kernel, out_shape=(square, square), in_specs=[whole...  5.51 us

profile of v2, /device:TPU:1, one launch (start us, length us, event | category | flops | bytes accessed | tf_op | source)
XLA Modules:
  0.0 96.3 jit_solution(4797701389116459817)
XLA Ops:
  0.6 0.0 copy-start
  0.6 0.7 copy-done
  1.3 54.3 %filter_gram.1 = (f32[3,16,128,128]{3,2,1,0:T(8,128)S(1)}, f32[8,16,128]{2,1,0:T(8,128)S(1)}) custom-call(f32[2048,128]{1,0:T(8,128)} %bitcast.1, s32[16,128]{1,0:T(8,128)S(1)} %copy-done), custom_call_target="tpu_custom_call" | custom-call | tf_op jit(solution)/shard_map/filter_gram/pallas_call | solution.py:470
  55.7 5.5 %factor.1 = (f32[128,128]{1,0:T(8,128)S(1)}, f32[128,128]{1,0:T(8,128)S(1)}) custom-call(f32[8,16,128]{2,1,0:T(8,128)S(1)} %get-tuple-element.9.gram_ref), custom_call_target="tpu_custom_call" | custom-call | tf_op jit(solution)/shard_map/factor/pallas_call | solution.py:486
  61.2 23.8 %basis_gram.1 = (f32[3,16,128,128]{3,2,1,0:T(8,128)S(1)}, f32[8,16,128]{2,1,0:T(8,128)S(1)}) custom-call(f32[3,16,128,128]{3,2,1,0:T(8,128)S(1)} %get-tuple-element.8.flat_ref, f32[128,128]{1,0:T(8,128)S(1)} %get-tuple-element.10.inverse_ref), custom_call_target="tpu_custom_call" | custom-call | tf_op jit(solution)/shard_map/basis_gram/pallas_call | solution.py:495
  85.0 11.1 %factor_modes.1 = (f32[128,3,16,128]{3,2,1,0:T(8,128)}, f32[128,128]{1,0:T(8,128)}) custom-call(f32[3,16,128,128]{3,2,1,0:T(8,128)S(1)} %get-tuple-element.11.basis, f32[8,16,128]{2,1,0:T(8,128)S(1)} %get-tuple-element.12.gram_ref, f32[128,128]{1,0:T(8,128)S(1)} %get-tuple-element.13.first_upper), custom_call_target="tpu_custom_call" | custom-call | tf_op jit(solution)/shard_map/factor_modes/pallas_call | solution.py:505
Async XLA Ops:
  0.6 0.7 copy-start

commit v3 on v2

--- a/solution.py
+++ b/solution.py
@@ -205,11 +205,11 @@
 
 def first_kernel(
     n_lon, n_lat,
-    p_hbm, mask_ref, flat, gram_ref,
-    p_ref, raw, masks, even, odd, quarter, keep_lon, keep_lat,
+    p_hbm, mask_hbm, flat, gram_ref,
+    p_ref, mask_ref, raw, masks, even, odd, quarter, keep_lon, keep_lat,
     part, slots_a, slots_y, slots_z, *sems,
 ):
-    reduce_sems, (near_send, near_recv, load_sem) = sems[:8], sems[8:]
+    reduce_sems, (near_send, near_recv, load_sem, mask_sem) = sems[:8], sems[8:]
     place = Place(n_lon, n_lat)
     clon, clat = mask_ref.shape
     snaps = raw.shape[2]
@@ -217,10 +217,13 @@
     rows = clon + 2 * MARGIN
     load = pltpu.make_async_copy(p_hbm, p_ref, load_sem)
     load.start()
+    load_mask = pltpu.make_async_copy(mask_hbm, mask_ref, mask_sem)
+    load_mask.start()
     sides = [place.near(0, 1), place.near(0, -1), place.near(1, 0), place.near(-1, 0)]
     expected = greet(sides + place.reduce_peers())
 
     own_lon, own_lat = pl.ds(BASE, clon), pl.ds(clat, clat)
+    load_mask.wait()
     masks[own_lon, own_lat] = mask_ref[...].astype(F32)
     load.wait()
 
@@ -256,7 +259,11 @@
             outer = pl.ds(at, MARGIN)
             number = 8 + 2 * index + end
             corners.append(near(number, raw.at[src, outer, :], raw.at[dst, outer, :], device))
-    for copy in lat_mask + lat_field + lon_field:
+    for copy in lat_mask + lat_field:
+        copy.start()
+    for copy in lat_field:
+        copy.wait_send()
+    for copy in lon_field:
         copy.start()
     for copy in lat_mask:
         copy.wait_recv()
@@ -290,14 +297,10 @@
         return 0
 
     lax.fori_loop(1, rows - 1, coefficients, 0)
-    for copy in lon_field + corners:
-        copy.wait_recv()
 
     def masked(row, _):
         even[row] = raw[row] * (4.0 * quarter[row])
         return 0
-
-    lax.fori_loop(0, rows, masked, 0)
 
     def sweep(source, target, row):
         scale = quarter[row]
@@ -305,14 +308,28 @@
         both = pltpu.roll(lon_swept, 1, 0) + pltpu.roll(lon_swept, wide - 1, 0)
         target[row] = lon_swept * keep_lat[row] + scale * both
 
-    for step in range(PASSES):
-        source, target = (even, odd) if step % 2 == 0 else (odd, even)
-
-        def one_row(row, _, source=source, target=target):
+    buffers = [(even, odd) if step % 2 == 0 else (odd, even) for step in range(PASSES)]
+    first, last = MARGIN, MARGIN + clon
+    lax.fori_loop(first, last, masked, 0)
+    for step, (source, target) in enumerate(buffers):
+
+        def inner_row(row, _, source=source, target=target):
             sweep(source, target, row)
             return 0
 
-        lax.fori_loop(1 + step, rows - 1 - step, one_row, 0)
+        lax.fori_loop(first + 1 + step, last - 1 - step, inner_row, 0)
+    for copy in lon_field + corners:
+        copy.wait_recv()
+    lax.fori_loop(0, first, masked, 0)
+    lax.fori_loop(last, rows, masked, 0)
+    for step, (source, target) in enumerate(buffers):
+
+        def outer_rows(row, _, source=source, target=target, step=step):
+            sweep(source, target, 1 + step + row)
+            sweep(source, target, last - 1 - step + row)
+            return 0
+
+        lax.fori_loop(0, MARGIN, outer_rows, 0)
     field = even if PASSES % 2 == 0 else odd
 
     def gradients(row, _):
@@ -334,7 +351,7 @@
     gram = gram_end(*lax.fori_loop(0, 3, gram_chunk, gram_start(snaps)))
     part[...] = gram.reshape(part.shape)
     all_reduce(place, part, slots_a, slots_y, slots_z, gram_ref, reduce_sems)
-    for copy in lat_mask + lat_field + lon_mask + lon_field + corners:
+    for copy in lat_mask + lon_mask + lon_field + corners:
         copy.wait_send()
 
 
@@ -384,9 +401,7 @@
         left = [row_of(left_work, at + i) for i in range(BLOCK)]
         right = [row_of(right_work, at + i) for i in range(BLOCK)]
         for j in range(BLOCK):
-            pivot = scalar[j, j]
-            root = lax.rsqrt(pivot)
-            root = root * (1.5 - 0.5 * pivot * root * root)
+            root = lax.rsqrt(scalar[j, j])
             below = {i: scalar[i, j] * root for i in range(j + 1, BLOCK)}
             left[j] = left[j] * root
             right[j] = right[j] * root
@@ -401,11 +416,13 @@
         done = at + BLOCK
         upper_ref[at:done, :] = panel[:, :n]
         inverse_ref[at:done, :] = panel[:, n:]
-        for low, high in ((done, done + BLOCK), (done + BLOCK, n)):
-            if low < high <= n:
-                change = exact_dot(panel[:, low:high], panel[...], 0, 0)
-                left_work[low:high, :] = left_work[low:high, :] - change[:, :n]
-                right_work[low:high, :] = right_work[low:high, :] - change[:, n:]
+        if done < n:
+            one, two, three = split(panel[...])
+            tall = jnp.concatenate([one, one, two, one, three, two], axis=0)
+            other = jnp.concatenate([one, two, one, three, one, two], axis=0)
+            change = multiply(tall[:, done:n], other, 0, 0)
+            left_work[done:, :] = left_work[done:, :] - change[:, :n]
+            right_work[done:, :] = right_work[done:, :] - change[:, n:]
     upper_ref[...] = jnp.where(columns >= rows, upper_ref[...], 0.0)
 
 
@@ -470,18 +487,20 @@
     field, gram = pl.pallas_call(
         functools.partial(first_kernel, n_lon, n_lat),
         out_shape=(flat, pieces),
-        in_specs=[whole(pltpu.HBM), whole()],
+        in_specs=[whole(pltpu.HBM), whole(pltpu.HBM)],
         out_specs=(whole(), whole()),
-        scratch_shapes=[pltpu.VMEM((snaps * clon, clat), F32), extended]
+        scratch_shapes=[pltpu.VMEM((snaps * clon, clat), F32)]
+        + [pltpu.VMEM((clon, clat), jnp.int32), extended]
         + [pltpu.VMEM((clon + 2 * BASE, 3 * clat), F32)]
         + 5 * [extended]
         + reduce_scratch(n_lon, n_lat, snaps)
         + 2 * [pltpu.SemaphoreType.DMA((12,))]
-        + [pltpu.SemaphoreType.DMA],
+        + 2 * [pltpu.SemaphoreType.DMA],
         compiler_params=params(32, 0),
         name="filter_gram",
     )(
-        pltpu.with_memory_space_constraint(pressure.reshape(snaps * clon, clat), pltpu.HBM), ocean_mask
+        pltpu.with_memory_space_constraint(pressure.reshape(snaps * clon, clat), pltpu.HBM),
+        pltpu.with_memory_space_constraint(ocean_mask, pltpu.HBM),
     )
     first_upper, first_inverse = pl.pallas_call(
         factor_kernel,

time: 96.5 us -> 93.2 us (0.966)
  Pallas kernels: 94.8 us -> 92.2 us
where the time goes in v3:
time: 93.2 us; the launch traced here: 93 us
  Pallas kernels  92.2 us (99%)
    pallas_call x1, Pallas kernels, on_device(): pl.pallas_call(functools.partial(first_kernel, n_lon, n_lat), out_shape=(...  53.5 us
    pallas_call x1, Pallas kernels, on_device(): pl.pallas_call(functools.partial(second_kernel, n_lon, n_lat), out_shape=...  23.5 us
    pallas_call x1, Pallas kernels, on_device(): pl.pallas_call(functools.partial(last_kernel, scale), out_shape=(jax.Shap...  10.4 us
    pallas_call x1, Pallas kernels, on_device(): pl.pallas_call(factor_kernel, out_shape=(square, square), in_specs=[whole...  4.84 us

profile of v3, /device:TPU:1, one launch (start us, length us, event | category | flops | bytes accessed | tf_op | source)
XLA Modules:
  0.0 93.0 jit_solution(14924330918875214723)
XLA Ops:
  0.6 53.5 %filter_gram.1 = (f32[3,16,128,128]{3,2,1,0:T(8,128)S(1)}, f32[8,16,128]{2,1,0:T(8,128)S(1)}) custom-call(f32[2048,128]{1,0:T(8,128)} %bitcast.1, s32[16,128]{1,0:T(8,128)} %mask_hbm.1), custom_call_target="tpu_custom_call" | custom-call | tf_op jit(solution)/shard_map/filter_gram/pallas_call | solution.py:487
  54.1 4.8 %factor.1 = (f32[128,128]{1,0:T(8,128)S(1)}, f32[128,128]{1,0:T(8,128)S(1)}) custom-call(f32[8,16,128]{2,1,0:T(8,128)S(1)} %get-tuple-element.9.gram_ref), custom_call_target="tpu_custom_call" | custom-call | tf_op jit(solution)/shard_map/factor/pallas_call | solution.py:505
  59.0 23.5 %basis_gram.1 = (f32[3,16,128,128]{3,2,1,0:T(8,128)S(1)}, f32[8,16,128]{2,1,0:T(8,128)S(1)}) custom-call(f32[3,16,128,128]{3,2,1,0:T(8,128)S(1)} %get-tuple-element.8.flat_ref, f32[128,128]{1,0:T(8,128)S(1)} %get-tuple-element.10.inverse_ref), custom_call_target="tpu_custom_call" | custom-call | tf_op jit(solution)/shard_map/basis_gram/pallas_call | solution.py:514
  82.5 10.4 %factor_modes.1 = (f32[128,3,16,128]{3,2,1,0:T(8,128)}, f32[128,128]{1,0:T(8,128)}) custom-call(f32[3,16,128,128]{3,2,1,0:T(8,128)S(1)} %get-tuple-element.11.basis, f32[8,16,128]{2,1,0:T(8,128)S(1)} %get-tuple-element.12.gram_ref, f32[128,128]{1,0:T(8,128)S(1)} %get-tuple-element.13.first_upper), custom_call_target="tpu_custom_call" | custom-call | tf_op jit(solution)/shard_map/factor_modes/pallas_call | solution.py:524

commit v4 on v3

--- a/solution.py
+++ b/solution.py
@@ -177,6 +177,13 @@
     main = multiply(jnp.concatenate([one, two], axis=1), wide[...], 1, 0)
     rest = multiply(jnp.concatenate([one, three], axis=1), narrow[...], 1, 0)
     return main[:, :columns] + (main[:, columns:] + rest)
+
+
+def apply_near_one(value, wide):
+    columns = value.shape[1]
+    one, two, _ = split(value)
+    main = multiply(jnp.concatenate([one, two], axis=1), wide[...], 1, 0)
+    return main[:, :columns] + main[:, columns:]
 
 
 def gram_parts(value):
@@ -318,18 +325,6 @@
             return 0
 
         lax.fori_loop(first + 1 + step, last - 1 - step, inner_row, 0)
-    for copy in lon_field + corners:
-        copy.wait_recv()
-    lax.fori_loop(0, first, masked, 0)
-    lax.fori_loop(last, rows, masked, 0)
-    for step, (source, target) in enumerate(buffers):
-
-        def outer_rows(row, _, source=source, target=target, step=step):
-            sweep(source, target, 1 + step + row)
-            sweep(source, target, last - 1 - step + row)
-            return 0
-
-        lax.fori_loop(0, MARGIN, outer_rows, 0)
     field = even if PASSES % 2 == 0 else odd
 
     def gradients(row, _):
@@ -342,13 +337,31 @@
         flat[2, row] = (half * (pltpu.roll(centre, wide - 1, 0) - pltpu.roll(centre, 1, 0)))[own]
         return 0
 
-    lax.fori_loop(0, clon, gradients, 0)
-
-    def gram_chunk(which, carry):
-        main, side = gram_parts(flat[which].reshape(clon * clat, snaps))
-        return carry[0] + main, carry[1] + side
-
-    gram = gram_end(*lax.fori_loop(0, 3, gram_chunk, gram_start(snaps)))
+    def add_gram(carry, *ranges):
+        for which in range(3):
+            values = [flat[which, low:high].reshape(-1, snaps) for low, high in ranges]
+            main, side = gram_parts(jnp.concatenate(values, axis=0))
+            carry = carry[0] + main, carry[1] + side
+        return carry
+
+    low_end, high_start = MARGIN, clon - MARGIN
+    lax.fori_loop(low_end, high_start, gradients, 0)
+    carry = add_gram(gram_start(snaps), (low_end, high_start))
+    for copy in lon_field + corners:
+        copy.wait_recv()
+    lax.fori_loop(0, first, masked, 0)
+    lax.fori_loop(last, rows, masked, 0)
+    for step, (source, target) in enumerate(buffers):
+
+        def outer_rows(row, _, source=source, target=target, step=step):
+            sweep(source, target, 1 + step + row)
+            sweep(source, target, last - 1 - step + row)
+            return 0
+
+        lax.fori_loop(0, MARGIN, outer_rows, 0)
+    lax.fori_loop(0, low_end, gradients, 0)
+    lax.fori_loop(high_start, clon, gradients, 0)
+    gram = gram_end(*add_gram(carry, (0, low_end), (high_start, clon)))
     part[...] = gram.reshape(part.shape)
     all_reduce(place, part, slots_a, slots_y, slots_z, gram_ref, reduce_sems)
     for copy in lat_mask + lon_mask + lon_field + corners:
@@ -363,7 +376,7 @@
     place = Place(n_lon, n_lat)
     expected = greet(place.reduce_peers())
     _, clon, clat, snaps = flat_ref.shape
-    group = 8
+    group = 16
     per = clon // group
     set_weights(inverse_ref[...].T, wide, narrow)
 
@@ -375,7 +388,7 @@
         main, side = gram_parts(value)
         return carry[0] + main, carry[1] + side
 
-    gram = gram_end(*lax.fori_loop(0, 3 * per, chunk, gram_start(snaps)))
+    gram = gram_end(*lax.fori_loop(0, 3 * per, chunk, gram_start(snaps), unroll=True))
     part[...] = gram.reshape(part.shape)
     pl.semaphore_wait(pltpu.get_barrier_semaphore(), expected)
     all_reduce(place, part, slots_a, slots_y, slots_z, gram_ref, sems)
@@ -447,13 +460,13 @@
     _, clon, clat, snaps = basis.shape
     factorize(gram_ref[...].reshape(upper.shape), *work, upper, inverse)
     set_weights(inverse[...].T * scale, wide, narrow)
-    group = 8
+    group = 4
     copies = []
     for which in range(3):
         for part in range(clon // group):
             start = part * group
             value = basis[which, start : start + group].reshape(group * clat, snaps)
-            value = apply_weights(value, wide, narrow)
+            value = apply_near_one(value, wide)
             for row in range(group):
                 staged[:, which, start + row, :] = value[row * clat : (row + 1) * clat].T
             here = (slice(None), which, pl.ds(start, group), slice(None))
@@ -528,7 +541,7 @@
         out_specs=(whole(pltpu.HBM), whole()),
         scratch_shapes=[pltpu.VMEM((snaps, snaps), F32)] * 2
         + weights
-        + [pltpu.VMEM((snaps, 3, clon, clat), F32), pltpu.SemaphoreType.DMA((6,))]
+        + [pltpu.VMEM((snaps, 3, clon, clat), F32), pltpu.SemaphoreType.DMA((3 * clon // 4,))]
         + factor_scratch(snaps),
         compiler_params=params(24),
         name="factor_modes",

time: 93.2 us -> 90.9 us (0.975)
  Pallas kernels: 92.2 us -> 89.9 us
    pallas_call x1, Pallas kernels: 23.5 us -> 22.2 us  [on_device(): pl.pallas_call(functools.partial(second_kernel, n_lon, n_lat), out_shape=...]
    pallas_call x1, Pallas kernels: 10.4 us -> 9.15 us  [on_device(): pl.pallas_call(functools.partial(last_kernel, scale), out_shape=(jax.Shap...]
where the time goes in v4:
time: 90.9 us; the launch traced here: 90.7 us
  Pallas kernels  89.9 us (99%)
    pallas_call x1, Pallas kernels, on_device(): pl.pallas_call(functools.partial(first_kernel, n_lon, n_lat), out_shape=(...  53.8 us
    pallas_call x1, Pallas kernels, on_device(): pl.pallas_call(functools.partial(second_kernel, n_lon, n_lat), out_shape=...  22.2 us
    pallas_call x1, Pallas kernels, on_device(): pl.pallas_call(functools.partial(last_kernel, scale), out_shape=(jax.Shap...  9.15 us
    pallas_call x1, Pallas kernels, on_device(): pl.pallas_call(factor_kernel, out_shape=(square, square), in_specs=[whole...  4.84 us

profile of v4, /device:TPU:1, one launch (start us, length us, event | category | flops | bytes accessed | tf_op | source)
XLA Modules:
  0.0 90.7 jit_solution(7559712225543529347)
XLA Ops:
  0.6 53.8 %filter_gram.1 = (f32[3,16,128,128]{3,2,1,0:T(8,128)S(1)}, f32[8,16,128]{2,1,0:T(8,128)S(1)}) custom-call(f32[2048,128]{1,0:T(8,128)} %bitcast.1, s32[16,128]{1,0:T(8,128)} %mask_hbm.1), custom_call_target="tpu_custom_call" | custom-call | tf_op jit(solution)/shard_map/filter_gram/pallas_call | solution.py:500
  54.4 4.8 %factor.1 = (f32[128,128]{1,0:T(8,128)S(1)}, f32[128,128]{1,0:T(8,128)S(1)}) custom-call(f32[8,16,128]{2,1,0:T(8,128)S(1)} %get-tuple-element.9.gram_ref), custom_call_target="tpu_custom_call" | custom-call | tf_op jit(solution)/shard_map/factor/pallas_call | solution.py:518
  59.3 22.2 %basis_gram.1 = (f32[3,16,128,128]{3,2,1,0:T(8,128)S(1)}, f32[8,16,128]{2,1,0:T(8,128)S(1)}) custom-call(f32[3,16,128,128]{3,2,1,0:T(8,128)S(1)} %get-tuple-element.8.flat_ref, f32[128,128]{1,0:T(8,128)S(1)} %get-tuple-element.10.inverse_ref), custom_call_target="tpu_custom_call" | custom-call | tf_op jit(solution)/shard_map/basis_gram/pallas_call | solution.py:527
  81.4 9.1 %factor_modes.1 = (f32[128,3,16,128]{3,2,1,0:T(8,128)}, f32[128,128]{1,0:T(8,128)}) custom-call(f32[3,16,128,128]{3,2,1,0:T(8,128)S(1)} %get-tuple-element.11.basis, f32[8,16,128]{2,1,0:T(8,128)S(1)} %get-tuple-element.12.gram_ref, f32[128,128]{1,0:T(8,128)S(1)} %get-tuple-element.13.first_upper), custom_call_target="tpu_custom_call" | custom-call | tf_op jit(solution)/shard_map/factor_modes/pallas_call | solution.py:537

commit v5 on v4

--- a/solution.py
+++ b/solution.py
@@ -226,7 +226,8 @@
     load.start()
     load_mask = pltpu.make_async_copy(mask_hbm, mask_ref, mask_sem)
     load_mask.start()
-    sides = [place.near(0, 1), place.near(0, -1), place.near(1, 0), place.near(-1, 0)]
+    around = [(a, b) for a in (1, 0, -1) for b in (1, 0, -1) if (a, b) != (0, 0)]
+    sides = [place.near(a, b) for a, b in around]
     expected = greet(sides + place.reduce_peers())
 
     own_lon, own_lat = pl.ds(BASE, clon), pl.ds(clat, clat)
@@ -245,42 +246,33 @@
     def near(index, source, target, device):
         return send(source, target, near_send.at[index], near_recv.at[index], device)
 
-    lat_mask, lat_field, lon_mask, lon_field, corners = [], [], [], [], []
+    mask_copies, lat_field, lon_field, corners = [], [], [], []
+    for index, (a, b) in enumerate(around):
+        src, dst = span(a, BASE, clon, MARGIN)
+        _, columns = span(b, clat, clat, clat)
+        source, target = masks.at[src, own_lat], masks.at[dst, columns]
+        mask_copies.append(near(8 + index, source, target, place.near(a, b)))
     for index, delta in enumerate((1, -1)):
-        device = place.near(0, delta)
-        src, dst = span(delta, clat, clat, clat)
-        lat_mask.append(
-            near(index, masks.at[own_lon, own_lat], masks.at[own_lon, dst], device)
-        )
         src, dst = span(delta, BASE, clat, MARGIN)
         inner = pl.ds(MARGIN, clon)
-        lat_field.append(near(2 + index, raw.at[inner, src, :], raw.at[inner, dst, :], device))
+        source, target = raw.at[inner, src, :], raw.at[inner, dst, :]
+        lat_field.append(near(index, source, target, place.near(0, delta)))
     for index, delta in enumerate((1, -1)):
         device = place.near(delta, 0)
-        src, dst = span(delta, BASE, clon, MARGIN)
-        lon_mask.append(near(4 + index, masks.at[src, :], masks.at[dst, :], device))
         src, dst = span(delta, MARGIN, clon, MARGIN)
         inner = pl.ds(BASE, clat)
-        lon_field.append(near(6 + index, raw.at[src, inner, :], raw.at[dst, inner, :], device))
+        lon_field.append(near(2 + index, raw.at[src, inner, :], raw.at[dst, inner, :], device))
         for end, at in enumerate((BASE - MARGIN, BASE + clat)):
             outer = pl.ds(at, MARGIN)
-            number = 8 + 2 * index + end
+            number = 4 + 2 * index + end
             corners.append(near(number, raw.at[src, outer, :], raw.at[dst, outer, :], device))
-    for copy in lat_mask + lat_field:
+    for copy in mask_copies + lat_field:
         copy.start()
     for copy in lat_field:
         copy.wait_send()
     for copy in lon_field:
         copy.start()
-    for copy in lat_mask:
-        copy.wait_recv()
-    for copy in lon_mask:
-        copy.start()
-    for copy in lat_field:
-        copy.wait_recv()
-    for copy in corners:
-        copy.start()
-    for copy in lon_mask:
+    for copy in mask_copies:
         copy.wait_recv()
 
     low = jnp.where(place.lat > 0, 1.0, 0.0)
@@ -304,6 +296,10 @@
         return 0
 
     lax.fori_loop(1, rows - 1, coefficients, 0)
+    for copy in lat_field:
+        copy.wait_recv()
+    for copy in corners:
+        copy.start()
 
     def masked(row, _):
         even[row] = raw[row] * (4.0 * quarter[row])
@@ -364,7 +360,7 @@
     gram = gram_end(*add_gram(carry, (0, low_end), (high_start, clon)))
     part[...] = gram.reshape(part.shape)
     all_reduce(place, part, slots_a, slots_y, slots_z, gram_ref, reduce_sems)
-    for copy in lat_mask + lon_mask + lon_field + corners:
+    for copy in mask_copies + lon_field + corners:
         copy.wait_send()
 
 
@@ -507,7 +503,7 @@
         + [pltpu.VMEM((clon + 2 * BASE, 3 * clat), F32)]
         + 5 * [extended]
         + reduce_scratch(n_lon, n_lat, snaps)
-        + 2 * [pltpu.SemaphoreType.DMA((12,))]
+        + 2 * [pltpu.SemaphoreType.DMA((16,))]
         + 2 * [pltpu.SemaphoreType.DMA],
         compiler_params=params(32, 0),
         name="filter_gram",

time: 90.9 us -> 88.7 us (0.976)
  Pallas kernels: 89.9 us -> 87.7 us
    pallas_call x1, Pallas kernels: 53.8 us -> 50.3 us  [on_device(): pl.pallas_call(functools.partial(first_kernel, n_lon, n_lat), out_shape=(...]
    pallas_call x1, Pallas kernels: 22.2 us -> 23.4 us  [on_device(): pl.pallas_call(functools.partial(second_kernel, n_lon, n_lat), out_shape=...]
where the time goes in v5:
time: 88.7 us; the launch traced here: 88.5 us
  Pallas kernels  87.7 us (99%)
    pallas_call x1, Pallas kernels, on_device(): pl.pallas_call(functools.partial(first_kernel, n_lon, n_lat), out_shape=(...  50.3 us
    pallas_call x1, Pallas kernels, on_device(): pl.pallas_call(functools.partial(second_kernel, n_lon, n_lat), out_shape=...  23.4 us
    pallas_call x1, Pallas kernels, on_device(): pl.pallas_call(functools.partial(last_kernel, scale), out_shape=(jax.Shap...  9.15 us
    pallas_call x1, Pallas kernels, on_device(): pl.pallas_call(factor_kernel, out_shape=(square, square), in_specs=[whole...  4.84 us

profile of v5, /device:TPU:1, one launch (start us, length us, event | category | flops | bytes accessed | tf_op | source)
XLA Modules:
  0.0 88.5 jit_solution(18036359458532956393)
XLA Ops:
  0.6 50.3 %filter_gram.1 = (f32[3,16,128,128]{3,2,1,0:T(8,128)S(1)}, f32[8,16,128]{2,1,0:T(8,128)S(1)}) custom-call(f32[2048,128]{1,0:T(8,128)} %bitcast.1, s32[16,128]{1,0:T(8,128)} %mask_hbm.1), custom_call_target="tpu_custom_call" | custom-call | tf_op jit(solution)/shard_map/filter_gram/pallas_call | solution.py:496
  51.0 4.8 %factor.1 = (f32[128,128]{1,0:T(8,128)S(1)}, f32[128,128]{1,0:T(8,128)S(1)}) custom-call(f32[8,16,128]{2,1,0:T(8,128)S(1)} %get-tuple-element.9.gram_ref), custom_call_target="tpu_custom_call" | custom-call | tf_op jit(solution)/shard_map/factor/pallas_call | solution.py:514
  55.8 23.4 %basis_gram.1 = (f32[3,16,128,128]{3,2,1,0:T(8,128)S(1)}, f32[8,16,128]{2,1,0:T(8,128)S(1)}) custom-call(f32[3,16,128,128]{3,2,1,0:T(8,128)S(1)} %get-tuple-element.8.flat_ref, f32[128,128]{1,0:T(8,128)S(1)} %get-tuple-element.10.inverse_ref), custom_call_target="tpu_custom_call" | custom-call | tf_op jit(solution)/shard_map/basis_gram/pallas_call | solution.py:523
  79.2 9.1 %factor_modes.1 = (f32[128,3,16,128]{3,2,1,0:T(8,128)}, f32[128,128]{1,0:T(8,128)}) custom-call(f32[3,16,128,128]{3,2,1,0:T(8,128)S(1)} %get-tuple-element.11.basis, f32[8,16,128]{2,1,0:T(8,128)S(1)} %get-tuple-element.12.gram_ref, f32[128,128]{1,0:T(8,128)S(1)} %get-tuple-element.13.first_upper), custom_call_target="tpu_custom_call" | custom-call | tf_op jit(solution)/shard_map/factor_modes/pallas_call | solution.py:533

commit v6 on v5

--- a/solution.py
+++ b/solution.py
@@ -354,9 +354,9 @@
             sweep(source, target, last - 1 - step + row)
             return 0
 
-        lax.fori_loop(0, MARGIN, outer_rows, 0)
-    lax.fori_loop(0, low_end, gradients, 0)
-    lax.fori_loop(high_start, clon, gradients, 0)
+        lax.fori_loop(0, MARGIN, outer_rows, 0, unroll=True)
+    lax.fori_loop(0, low_end, gradients, 0, unroll=True)
+    lax.fori_loop(high_start, clon, gradients, 0, unroll=True)
     gram = gram_end(*add_gram(carry, (0, low_end), (high_start, clon)))
     part[...] = gram.reshape(part.shape)
     all_reduce(place, part, slots_a, slots_y, slots_z, gram_ref, reduce_sems)

time: 88.7 us -> 88.5 us (level)
  no operation moved by 1% of the time
where the time goes in v6:
time: 88.5 us; the launch traced here: 88.3 us
  Pallas kernels  87.5 us (99%)
    pallas_call x1, Pallas kernels, on_device(): pl.pallas_call(functools.partial(first_kernel, n_lon, n_lat), out_shape=(...  49.9 us
    pallas_call x1, Pallas kernels, on_device(): pl.pallas_call(functools.partial(second_kernel, n_lon, n_lat), out_shape=...  23.4 us
    pallas_call x1, Pallas kernels, on_device(): pl.pallas_call(functools.partial(last_kernel, scale), out_shape=(jax.Shap...  9.36 us
    pallas_call x1, Pallas kernels, on_device(): pl.pallas_call(factor_kernel, out_shape=(square, square), in_specs=[whole...  4.84 us

profile of v6, /device:TPU:1, one launch (start us, length us, event | category | flops | bytes accessed | tf_op | source)
XLA Modules:
  0.0 88.3 jit_solution(2485583338601575402)
XLA Ops:
  0.6 49.9 %filter_gram.1 = (f32[3,16,128,128]{3,2,1,0:T(8,128)S(1)}, f32[8,16,128]{2,1,0:T(8,128)S(1)}) custom-call(f32[2048,128]{1,0:T(8,128)} %bitcast.1, s32[16,128]{1,0:T(8,128)} %mask_hbm.1), custom_call_target="tpu_custom_call" | custom-call | tf_op jit(solution)/shard_map/filter_gram/pallas_call | solution.py:496
  50.6 4.8 %factor.1 = (f32[128,128]{1,0:T(8,128)S(1)}, f32[128,128]{1,0:T(8,128)S(1)}) custom-call(f32[8,16,128]{2,1,0:T(8,128)S(1)} %get-tuple-element.9.gram_ref), custom_call_target="tpu_custom_call" | custom-call | tf_op jit(solution)/shard_map/factor/pallas_call | solution.py:514
  55.4 23.4 %basis_gram.1 = (f32[3,16,128,128]{3,2,1,0:T(8,128)S(1)}, f32[8,16,128]{2,1,0:T(8,128)S(1)}) custom-call(f32[3,16,128,128]{3,2,1,0:T(8,128)S(1)} %get-tuple-element.8.flat_ref, f32[128,128]{1,0:T(8,128)S(1)} %get-tuple-element.10.inverse_ref), custom_call_target="tpu_custom_call" | custom-call | tf_op jit(solution)/shard_map/basis_gram/pallas_call | solution.py:523
  78.8 9.4 %factor_modes.1 = (f32[128,3,16,128]{3,2,1,0:T(8,128)}, f32[128,128]{1,0:T(8,128)}) custom-call(f32[3,16,128,128]{3,2,1,0:T(8,128)S(1)} %get-tuple-element.11.basis, f32[8,16,128]{2,1,0:T(8,128)S(1)} %get-tuple-element.12.gram_ref, f32[128,128]{1,0:T(8,128)S(1)} %get-tuple-element.13.first_upper), custom_call_target="tpu_custom_call" | custom-call | tf_op jit(solution)/shard_map/factor_modes/pallas_call | solution.py:533
